TPU v7x, 32 devices: a whole 2x2x4 slice. The times are simulated.
32 devices in a mesh: seq: 4 (over y, x), mp: 8 (over z, core).
Axes of the slice: x: 2, y: 2, z: 4, core: 2. Of those that a mesh axis runs over, the one named last changes fastest.
Arguments:
- incoming: bfloat16 [2048, 4096], P('seq', 'mp'), may hold values from -12 to 12
- queries: bfloat16 [2048, 4096], P('seq', 'mp'), may hold values from -5 to 5
- key_vecs: bfloat16 [2048, 4096], P('seq', 'mp'), may hold values from -5 to 5
- value_vecs: bfloat16 [2048, 4096], P('seq', 'mp'), may hold values from -6 to 6
- w_out: bfloat16 [4096, 4096], P(None, 'mp'), may hold values from -0.09375 to 0.09375
- norm_gain: float32 [4096], P('mp'), may hold values from 0.25 to 1.75
- filters: bfloat16 [4096, 256], P('mp'), may hold values from -0.375 to 0.375
- filter_len: int32 [4096], P('mp'), may hold values from 128 to 256, as said below
- skip_gain: float32 [4096], P('mp'), may hold values from 0.5 to 1.5
- slot_map: int32 [8], replicated, may hold values from 0 to 7, as said below
Outputs:
- layer_out: bfloat16 [2048, 4096], P('seq', 'mp')
Inputs may be any that keep to these rules, and one draw needn't show every extreme that they name: `slot_map`: slots 2 * i and 2 * i + 1, the rows of index i of seq, hold blocks i and 7 - i, in either order. `filter_len`: some channel uses all 256 taps.
All inputs are finite; a program needn't handle non-finite values.
Results may differ from a plain program's by a relative error of at most 0.0055.
Values may be sent and summed in bfloat16 or wider, within the bound.
No kernel may reach another device: no remote copies, remote signals or barrier semaphores. Data moves between devices by JAX's collectives and lax.ppermute only.
A program may use at most 64 MiB of HBM per device.

v0:
```python
import functools

import jax
import jax.numpy as jnp
import numpy as np
from jax import lax
from jax.experimental import pallas as pl
from jax.experimental.pallas import tpu as pltpu
from jax.sharding import PartitionSpec as P


HD = 128
EPS = 1e-05
NEG = -1e30
LOG2E = 1.4426950408889634
BF = jnp.bfloat16
F32 = jnp.float32
VMEM = pltpu.VMEM
SMEM = pltpu.SMEM


def shifted(block, axis, distance):
    devices = range(lax.axis_size(axis))
    route = [(i - distance, i) for i in devices if i - distance in devices]
    return lax.ppermute(block, axis, route)


def block_update(running, query_heads, query_pos, key_part, value_part, key_pos):
    peak_now, total_now, accum_now = running
    key_count = key_part.shape[0]
    head_count = query_heads.shape[1]
    key_heads = key_part.reshape(key_count, head_count, HD)
    value_heads = value_part.reshape(key_count, head_count, HD)
    scores = jnp.einsum(
        "thd,shd->ths", query_heads, key_heads, preferred_element_type=F32
    ) * HD ** (-0.5)
    allowed = key_pos[None, None, :] <= query_pos[:, None, None]
    masked = jnp.where(allowed, scores, NEG)
    peak_next = jnp.maximum(peak_now, jnp.max(masked, axis=2))
    weights = jnp.where(allowed, jnp.exp(masked - peak_next[:, :, None]), 0.0)
    factor = jnp.exp(peak_now - peak_next)
    total_next = total_now * factor + jnp.sum(weights, axis=2)
    summed = jnp.einsum(
        "ths,shd->thd", weights.astype(BF), value_heads, preferred_element_type=F32
    )
    return (peak_next, total_next, accum_now * factor[:, :, None] + summed)


def attend_keys(running, query_heads, query_pos, key_part, value_part, key_pos, block_rows):
    block_count = key_part.shape[0] // block_rows

    def attend_advance(state, item):
        return block_update(state, query_heads, query_pos, *item), None

    stacked = (
        key_part.reshape(block_count, block_rows, -1),
        value_part.reshape(block_count, block_rows, -1),
        key_pos.reshape(block_count, block_rows),
    )
    running, _ = lax.scan(attend_advance, running, stacked)
    return running


def causal_window(extended, taps_lag):
    pair_count, twice, width = extended.shape
    length = twice // 2
    tap_count = taps_lag.shape[0]
    inner = int(np.gcd(tap_count, 16))

    def causal_advance(block, accum):
        base = block * inner
        window = lax.dynamic_slice_in_dim(
            extended, length - base - inner + 1, length + inner - 1, 1
        ).astype(F32)
        tap_block = lax.dynamic_slice_in_dim(taps_lag, base, inner, 0).astype(F32)
        for lag in range(inner):
            offset = inner - 1 - lag
            accum = accum + tap_block[lag][None, None, :] * window[:, offset : offset + length]
        return accum

    start = jnp.zeros((pair_count, length, width), F32)
    return lax.fori_loop(0, tap_count // inner, causal_advance, start)


def general_device(
    incoming, queries, key_vecs, value_vecs, w_out, norm_gain, filters, filter_len, skip_gain, slot_map
):
    tok_rows, local_width = queries.shape
    span_rows = tok_rows // 2
    head_count = local_width // HD
    model_width = w_out.shape[0]
    all_rows = slot_map.shape[0] * span_rows
    row_ids = jnp.arange(all_rows, dtype=jnp.int32)
    position = (
        jnp.repeat(slot_map, span_rows, total_repeat_length=all_rows) * span_rows
        + row_ids % span_rows
    )
    seq_rank = lax.axis_index("seq")
    seq_size = lax.axis_size("seq")
    own_pos = lax.dynamic_slice_in_dim(position, seq_rank * tok_rows, tok_rows)
    query_heads = queries.reshape(tok_rows, head_count, HD)
    keys_all = lax.all_gather(key_vecs, "seq", axis=0, tiled=True)
    values_all = lax.all_gather(value_vecs, "seq", axis=0, tiled=True)
    running = attend_keys(
        (
            jnp.full((tok_rows, head_count), NEG, F32),
            jnp.zeros((tok_rows, head_count), F32),
            jnp.zeros((tok_rows, head_count, HD), F32),
        ),
        query_heads,
        own_pos,
        keys_all,
        values_all,
        position,
        2 * tok_rows,
    )
    attention = (running[2] / running[1][:, :, None]).reshape(-1, local_width).astype(BF)
    projected = jnp.dot(
        lax.all_gather(attention, "mp", axis=1, tiled=True), w_out, preferred_element_type=F32
    )
    residual = incoming.astype(F32) + projected
    square_total = lax.psum(jnp.sum(residual * residual, axis=1), "mp")
    scale = lax.rsqrt(square_total / model_width + EPS)
    normed = (residual * scale[:, None] * norm_gain[None, :]).astype(BF)
    tap_count = filters.shape[1]
    taps = jnp.where(
        jnp.arange(tap_count, dtype=jnp.int32)[None, :] < filter_len[:, None],
        filters,
        jnp.zeros((), filters.dtype),
    )
    pair_ids = lax.dynamic_slice_in_dim(slot_map, 2 * seq_rank, 2)
    low_first = pair_ids[0] < pair_ids[1]
    slots = normed.reshape(2, span_rows, local_width)
    low_rows = jnp.where(low_first, slots[0], slots[1])
    high_rows = jnp.where(low_first, slots[1], slots[0])
    own_pair = jnp.stack([low_rows, high_rows])
    low_before = shifted(low_rows, "seq", 1)
    high_before = shifted(high_rows, "seq", -1)
    high_before = jnp.where(seq_rank == seq_size - 1, low_rows, high_before)
    before_pair = jnp.stack([low_before, high_before])
    conv_pair = causal_window(jnp.concatenate([before_pair, own_pair], axis=1), taps.T)
    conv_slots = jnp.where(low_first, conv_pair, conv_pair[::-1])
    conv_rows = conv_slots.reshape(tok_rows, local_width)
    layer_out = residual + conv_rows + skip_gain[None, :] * normed.astype(F32)
    return layer_out.astype(BF)


def params(megabytes=20):
    return pltpu.CompilerParams(vmem_limit_bytes=megabytes << 20)


def cost(flops, moved, exps=0):
    return pl.CostEstimate(flops=int(flops), bytes_accessed=int(moved), transcendentals=int(exps))


def vm():
    return pl.BlockSpec(memory_space=VMEM)


def sm():
    return pl.BlockSpec(memory_space=SMEM)


def xor_route(count, k):
    return [(i, i ^ k) for i in range(count)]


def half_index(slots_ref, ids_ref, high):
    rank = ids_ref[0]
    first_is_high = slots_ref[2 * rank] > slots_ref[2 * rank + 1]
    return jnp.where(first_is_high, 1 - high, high).astype(jnp.int32)


def pack_kernel(n, high, slots_ref, ids_ref, q_ref, k_ref, v_ref, *rest):
    outs, sem = rest[:n], rest[n]
    rank = ids_ref[0]
    rows = outs[0].shape[0] // 3
    wide = outs[0].shape[1]
    half = half_index(slots_ref, ids_ref, high)
    source_rows = pl.ds(pl.multiple_of(half * rows, rows), rows)
    copies = []
    for k in range(n):
        cols = pl.ds(pl.multiple_of((rank ^ k) * wide, wide), wide)
        for a, ref in enumerate((q_ref, k_ref, v_ref)):
            copy = pltpu.make_async_copy(
                ref.at[source_rows, cols],
                outs[k].at[a * rows : (a + 1) * rows, :],
                sem.at[k, a],
            )
            copy.start()
            copies.append(copy)
    for copy in copies:
        copy.wait()


def in_hbm(array):
    return pltpu.with_memory_space_constraint(array, pltpu.HBM)


def pack(n, high, slots, ids, arrays):
    rows, width = arrays[0].shape[0] // 2, arrays[0].shape[1]
    piece = jax.ShapeDtypeStruct((3 * rows, width // n), BF)
    return pl.pallas_call(
        functools.partial(pack_kernel, n, high),
        out_shape=[piece] * n,
        in_specs=[sm(), sm()] + [pl.BlockSpec(memory_space=pltpu.HBM)] * 3,
        out_specs=[vm()] * n,
        scratch_shapes=[pltpu.SemaphoreType.DMA((n, 3))],
        compiler_params=params(8),
        cost_estimate=cost(0, 12 * rows * width),
    )(in_hbm(slots), ids, *(in_hbm(x) for x in arrays))


def attend_kernel(n, high, rows, ids_ref, *refs):
    chunks = 2 if high else 1
    ins = refs[: chunks * n]
    outs = refs[chunks * n : chunks * n + n]
    q_all, k_all, v_all, o_all = refs[chunks * n + n :]
    rank = ids_ref[0]
    wide = outs[0].shape[1]

    def place(block):
        return pl.ds(pl.multiple_of(block * rows, rows), rows)

    for c in range(chunks):
        for k in range(n):
            source = rank ^ k
            block = source if c == 0 else 2 * n - 1 - source
            piece = ins[c * n + k]
            if c == chunks - 1:
                q_all[place(block - c * n), :] = piece[0:rows, :]
            k_all[place(block), :] = piece[rows : 2 * rows, :]
            v_all[place(block), :] = piece[2 * rows : 3 * rows, :]
    base = n if high else 0
    row_id = lax.broadcasted_iota(jnp.int32, (rows, rows), 0)
    col_id = lax.broadcasted_iota(jnp.int32, (rows, rows), 1)
    causal = col_id <= row_id
    factor = HD ** (-0.5) * LOG2E
    nt = (((1,), (1,)), ((), ()))
    for b in range(n):
        past = (base + b) * rows
        for h in range(wide // HD):
            cols = slice(h * HD, (h + 1) * HD)
            q = q_all[b * rows : (b + 1) * rows, cols]
            near = lax.dot_general(
                q, k_all[past : past + rows, cols], nt, preferred_element_type=F32
            )
            near = jnp.where(causal, near, NEG)
            peak = jnp.max(near, axis=1, keepdims=True)
            if past:
                far = lax.dot_general(q, k_all[0:past, cols], nt, preferred_element_type=F32)
                peak = jnp.maximum(peak, jnp.max(far, axis=1, keepdims=True))
            w_near = jnp.exp2((near - peak) * factor)
            total = jnp.sum(w_near, axis=1, keepdims=True)
            summed = jnp.dot(
                w_near.astype(BF), v_all[past : past + rows, cols], preferred_element_type=F32
            )
            if past:
                w_far = jnp.exp2((far - peak) * factor)
                total = total + jnp.sum(w_far, axis=1, keepdims=True)
                summed = summed + jnp.dot(
                    w_far.astype(BF), v_all[0:past, cols], preferred_element_type=F32
                )
            owner = n - 1 - b if high else b
            o_all[owner * rows : (owner + 1) * rows, cols] = (summed / total).astype(BF)
    for k in range(n):
        outs[k][...] = o_all[place(rank ^ k), :]


def attend(n, high, rows, ids, pieces):
    wide = pieces[0].shape[1]
    chunks = 2 if high else 1
    pairs = n * (n + 1) // 2 + (n * n if high else 0)
    area = pairs * rows * rows * (wide // HD)
    return pl.pallas_call(
        functools.partial(attend_kernel, n, high, rows),
        out_shape=[jax.ShapeDtypeStruct((rows, wide), BF)] * n,
        in_specs=[sm()] + [vm()] * len(pieces),
        out_specs=[vm()] * n,
        scratch_shapes=[
            VMEM((n * rows, wide), BF),
            VMEM((chunks * n * rows, wide), BF),
            VMEM((chunks * n * rows, wide), BF),
            VMEM((n * rows, wide), BF),
        ],
        compiler_params=params(32),
        cost_estimate=cost(4 * area * HD, 8 * n * rows * wide * chunks, area),
        name="attend_high" if high else "attend_low",
    )(ids, *pieces)


def project_kernel(n, high, indices, has_low, slots_ref, ids_ref, base_ref, w_ref, *refs):
    count = len(indices)
    parts, outs, lhs = refs[:count], refs[count + has_low : -1], refs[-1]
    rank = ids_ref[0]
    me = ids_ref[1]
    rows, width = lhs.shape
    wide = width // n
    if base_ref.dtype == F32:
        total = base_ref[...]
    else:
        half = half_index(slots_ref, ids_ref, high)
        total = base_ref[pl.ds(pl.multiple_of(half * rows, rows), rows), :].astype(F32)
    for index, part in zip(indices, parts):
        for k in range(n):
            cols = pl.ds(pl.multiple_of((rank ^ k) * wide, wide), wide)
            lhs[:, cols] = part[k * rows : (k + 1) * rows, :]
        depth = pl.ds(pl.multiple_of((me ^ index) * width, width), width)
        total = total + jnp.dot(lhs[...], w_ref[depth, :], preferred_element_type=F32)
    outs[0][...] = total
    if len(outs) == 1:
        return
    outs[1][...] = total.astype(BF)
    squares = total * total
    lanes = squares[:, 0:HD]
    for g in range(1, squares.shape[1] // HD):
        lanes = lanes + squares[:, g * HD : (g + 1) * HD]
    if has_low:
        outs[2][:, 0:rows] = refs[count][...]
        outs[2][:, rows : 2 * rows] = jnp.sum(lanes.T, axis=0, keepdims=True)
    else:
        outs[2][...] = jnp.sum(lanes.T, axis=0, keepdims=True)


def project(n, high, slots, ids, base, w_out, parts, indices, final, low_squares=()):
    rows, width = parts[0].shape[0] // n, w_out.shape[1]
    shapes = [jax.ShapeDtypeStruct((rows, width), F32)]
    extra = list(low_squares)
    if final:
        shapes.append(jax.ShapeDtypeStruct((rows, width), BF))
        shapes.append(jax.ShapeDtypeStruct((1, rows * (1 + len(extra))), F32))
    return pl.pallas_call(
        functools.partial(project_kernel, n, high, indices, len(extra)),
        out_shape=shapes,
        in_specs=[sm(), sm()] + [vm()] * (2 + len(parts) + len(extra)),
        out_specs=[vm()] * len(shapes),
        scratch_shapes=[VMEM((rows, width), BF)],
        compiler_params=params(20),
        cost_estimate=cost(2 * rows * width * width * len(parts), 2 * w_out.size * 1.5),
    )(slots, ids, base, w_out, *parts, *extra)


def normed_rows(res, sq_row, gain, model_width):
    rows, width = res.shape
    scale = lax.rsqrt(sq_row / model_width + EPS)
    column = jnp.broadcast_to(scale, (HD, rows)).T
    parts = [
        (res[:, g * HD : (g + 1) * HD] * column * gain[:, g * HD : (g + 1) * HD]).astype(BF)
        for g in range(width // HD)
    ]
    return jnp.concatenate(parts, axis=1)


def split(array):
    high = array.astype(jnp.bfloat16)
    low = (array - high.astype(np.float64)).astype(jnp.bfloat16)
    return high, low


def transform_tables(rows):
    size = 2 * rows
    freq = np.arange(rows)[:, None].astype(np.float64)
    time = np.arange(rows)[None, :].astype(np.float64)
    angle = 2 * np.pi * ((freq * time) % size) / size
    cosine = np.cos(angle)
    sine = -np.sin(angle)
    nyquist = np.where(np.arange(rows) % 2 == 0, 1.0, -1.0)
    sine[0] = nyquist
    forward = np.concatenate([cosine, sine], axis=0)
    late = 2 * np.pi * ((freq * (time + rows)) % size) / size
    back_cos = 2 * np.cos(late)
    back_cos[0] = 1.0
    back_sin = -2 * np.sin(late)
    back_sin[0] = np.where((np.arange(rows) + rows) % 2 == 0, 1.0, -1.0)
    backward = np.concatenate([back_cos, back_sin], axis=0).T / size
    return split(forward), split(backward)


def spectrum_kernel(filters_ref, len_ref, fh_ref, fl_ref, out_ref):
    taps = filters_ref.shape[1]
    lag = lax.broadcasted_iota(jnp.int32, filters_ref.shape, 1)
    used = jnp.where(lag < len_ref[...], filters_ref[...].astype(F32), 0.0).astype(BF)
    nt = (((1,), (1,)), ((), ()))
    fh = fh_ref[:, 0:taps]
    fl = fl_ref[:, 0:taps]
    out_ref[...] = lax.dot_general(fh, used, nt, preferred_element_type=F32) + lax.dot_general(
        fl, used, nt, preferred_element_type=F32
    )


def spectrum(filters, filter_len, forward):
    return pl.pallas_call(
        spectrum_kernel,
        out_shape=jax.ShapeDtypeStruct((forward[0].shape[0], filters.shape[0]), F32),
        in_specs=[vm()] * 4,
        out_specs=vm(),
        compiler_params=params(12),
        cost_estimate=cost(4 * forward[0].size * filters.shape[0], 8 * filters.size),
        name="spectrum",
    )(filters, filter_len.reshape(-1, 1), *forward)


def two(a_high, a_low, b):
    return jnp.dot(a_high, b, preferred_element_type=F32) + jnp.dot(
        a_low, b, preferred_element_type=F32
    )


def frequency_signs(rows):
    row_id = lax.broadcasted_iota(jnp.int32, (rows, 1), 0)
    return row_id == 0, jnp.where(row_id % 2 == 0, 1.0, -1.0)


def late_spectrum(own, fh, fl):
    rows = own.shape[0]
    first, sign = frequency_signs(rows)
    plain = two(fh, fl, own)
    return sign * plain[:rows], jnp.where(first, 1.0, sign) * plain[rows:]


def filtered_spectrum(x_re, x_im, spec):
    rows = x_re.shape[0]
    first, _ = frequency_signs(rows)
    h_re, h_im = spec[:rows], spec[rows:]
    h_cross = jnp.where(first, 0.0, h_im)
    h_own = jnp.where(first, h_im, h_re)
    return jnp.concatenate([x_re * h_re - x_im * h_cross, x_re * h_cross + x_im * h_own], axis=0)


def filtered(x_re, x_im, gh, gl, spec):
    y = filtered_spectrum(x_re, x_im, spec)
    y_high = y.astype(BF)
    y_low = (y - y_high.astype(F32)).astype(BF)
    return two(gh, gl, y_high) + jnp.dot(gh, y_low, preferred_element_type=F32)


def conv_own_kernel(
    model_width, res_low, res_high, sq_ref, spec_ref, gain_ref, skip_ref, fh, fl, gh, gl,
    out_ref, low_ref,
):
    rows = spec_ref.shape[0] // 2
    for high, res_ref in enumerate((res_low, res_high)):
        part = slice(high * rows, (high + 1) * rows)
        res = res_ref[...]
        own = normed_rows(res, sq_ref[:, part], gain_ref[...], model_width)
        if not high:
            low_ref[...] = own
        late_re, late_im = late_spectrum(own, fh[...], fl[...])
        conv = filtered(late_re, late_im, gh[...], gl[...], spec_ref[...])
        out_ref[part, :] = res + conv + skip_ref[...] * own.astype(F32)


def conv_last_kernel(
    n, model_width, slots_ref, ids_ref, part_ref, low_ref, raw_low, raw_high, sq_a, sq_b,
    spec_ref, gain_ref, fh, gh, out_ref,
):
    rows = low_ref.shape[0]
    rank = ids_ref[0]
    odd = rank % 2 == 1
    for high, raw_ref in enumerate((raw_low, raw_high)):
        part = slice(high * rows, (high + 1) * rows)
        squares = jnp.where(odd != (high == 1), sq_a[:, part], sq_b[:, part])
        before = normed_rows(raw_ref[...].astype(F32), squares, gain_ref[...], model_width)
        before = before.astype(F32)
        if high:
            before = jnp.where(rank == n - 1, low_ref[...].astype(F32), before).astype(BF)
        else:
            before = jnp.where(rank == 0, 0.0, before).astype(BF)
        early = jnp.dot(fh[...], before, preferred_element_type=F32)
        y = filtered_spectrum(early[:rows], early[rows:], spec_ref[...]).astype(BF)
        conv = jnp.dot(gh[...], y, preferred_element_type=F32)
        half = half_index(slots_ref, ids_ref, high)
        out_ref[pl.ds(pl.multiple_of(half * rows, rows), rows), :] = (part_ref[part, :] + conv).astype(
            BF
        )


def relayed_piece(own, near, size):
    inner = [(i, i ^ (size - 2)) for i in range(2, size - 2)]
    direct = lax.ppermute(own, "mp", inner)
    ends = [(2, 0), (3, 1), (size - 4, size - 2), (size - 3, size - 1)]
    return direct + lax.ppermute(near, "mp", ends)


def gather_mp(own, size, relay):
    chips = size // 2
    pieces = [own]
    for k in range(1, chips):
        if relay and k == chips - 1:
            pieces.append(relayed_piece(own, pieces[k - 1], size))
        else:
            pieces.append(lax.ppermute(own, "mp", xor_route(size, 2 * k)))
    parts = []
    for piece in pieces:
        parts.append(piece)
        parts.append(lax.ppermute(piece, "mp", xor_route(size, 1)))
    return parts


def total_mp(part, size):
    k = 1
    while k < size:
        part = part + lax.ppermute(part, "mp", xor_route(size, k))
        k *= 2
    return part


def ring(n, step):
    return [(i, (i + step) % n) for i in range(n)]


def pairs(n, offset):
    route = []
    for i in range(offset, n, 2):
        route += [(i, (i + 1) % n), ((i + 1) % n, i)]
    return route


def fast_device(
    incoming, queries, key_vecs, value_vecs, w_out, norm_gain, filters, filter_len, skip_gain, slot_map
):
    n = lax.axis_size("seq")
    mp_size = lax.axis_size("mp")
    rows, width = queries.shape[0] // 2, queries.shape[1]
    model_width = w_out.shape[0]
    ids = jnp.stack([lax.axis_index("seq"), lax.axis_index("mp")]).astype(jnp.int32)
    gain = norm_gain.reshape(1, -1)
    skip = skip_gain.reshape(1, -1)
    forward, backward = transform_tables(rows)
    forward = tuple(jnp.asarray(t) for t in forward)
    backward = tuple(jnp.asarray(t) for t in backward)

    def exchange(pieces):
        return [pieces[0]] + [lax.ppermute(pieces[k], "seq", xor_route(n, k)) for k in range(1, n)]

    inputs = (queries, key_vecs, value_vecs)
    low = exchange(pack(n, 0, slot_map, ids, inputs))
    high = exchange(pack(n, 1, slot_map, ids, inputs))
    spec = spectrum(filters, filter_len, forward)

    att_low = exchange(attend(n, 0, rows, ids, low))
    parts_low = gather_mp(jnp.concatenate(att_low, axis=0), mp_size, True)
    att_high = exchange(attend(n, 1, rows, ids, low + high))
    parts_high = gather_mp(jnp.concatenate(att_high, axis=0), mp_size, False)

    most = mp_size // 2
    every = tuple(range(mp_size))
    res_low, raw_low, sq_low = project(n, 0, slot_map, ids, incoming, w_out, parts_low, every, True)
    raw_low = lax.ppermute(raw_low, "seq", ring(n, 1))
    (base,) = project(
        n, 1, slot_map, ids, incoming, w_out,
        parts_high[:most], every[:most], False,
    )
    res_high, raw_high, squares = project(
        n, 1, slot_map, ids, base, w_out,
        parts_high[most:], every[most:], True, (sq_low,),
    )
    raw_high = lax.ppermute(raw_high, "seq", ring(n, -1))
    squares = total_mp(squares, mp_size)
    sq_a = lax.ppermute(squares, "seq", pairs(n, 0))
    sq_b = lax.ppermute(squares, "seq", pairs(n, 1))
    transforms = forward + backward
    part, norm_low = pl.pallas_call(
        functools.partial(conv_own_kernel, model_width),
        out_shape=[
            jax.ShapeDtypeStruct((2 * rows, width), F32),
            jax.ShapeDtypeStruct((rows, width), BF),
        ],
        in_specs=[vm()] * 10,
        out_specs=[vm()] * 2,
        compiler_params=params(20),
        cost_estimate=cost(20 * rows * rows * width, 24 * rows * width),
        name="conv_own",
    )(res_low, res_high, squares, spec, gain, skip, *transforms)
    return pl.pallas_call(
        functools.partial(conv_last_kernel, n, model_width),
        out_shape=jax.ShapeDtypeStruct((2 * rows, width), BF),
        in_specs=[sm(), sm()] + [vm()] * 10,
        out_specs=vm(),
        compiler_params=params(20),
        cost_estimate=cost(20 * rows * rows * width, 24 * rows * width),
        name="conv_last",
    )(
        slot_map, ids, part, norm_low, raw_low, raw_high, sq_a, sq_b, spec, gain, forward[0], backward[0]
    )


def power_of_two(value):
    return value & (value - 1) == 0


def on_device(*arrays):
    n = lax.axis_size("seq")
    size = lax.axis_size("mp")
    queries, filters = arrays[1], arrays[6]
    rows = queries.shape[0] // 2
    heads = queries.shape[1] // HD
    fits = (
        heads % n == 0
        and power_of_two(n)
        and power_of_two(size)
        and n % 2 == 0
        and size >= 8
        and rows % 256 == 0
        and filters.shape[1] <= rows
    )
    if not fits:
        return general_device(*arrays)
    return fast_device(*arrays)


def solution(mesh):
    placed = (
        P("seq", "mp"),
        P("seq", "mp"),
        P("seq", "mp"),
        P("seq", "mp"),
        P(None, "mp"),
        P("mp"),
        P("mp", None),
        P("mp"),
        P("mp"),
        P(),
    )
    return jax.shard_map(
        on_device, mesh=mesh, in_specs=placed, out_specs=P("seq", "mp"), check_vma=False
    )
```

profile of v0, /device:TPU:0, one launch (start us, length us, event | category | flops | bytes accessed | tf_op | source)
XLA Modules:
  0.0 104.5 jit_solution(3087954455255899525)
XLA Ops:
  0.0 0.1 pad_add_fusion.ids_ref
  0.1 2.0 %shard_map.136 = (bf16[768,128]{1,0:T(8,128)(2,1)S(1)}, bf16[768,128]{1,0:T(8,128)(2,1)S(1)}, bf16[768,128]{1,0:T(8,128)(2,1)S(1)}, bf16[768,128]{1,0:T(8,128)(2,1)S(1)}) custom-call(s32[8]{0:T(128)} %slots_ref.11, s32[2]{0:T(128)S(1)} %pad_add_fusion.ids_ref, bf16[512,512]{1,0:T(8,128)(2,1)} %q_ref.3, bf16[512,512]{1,0:T(8,128)(2,1)} %k_ref.3, ...), custom_call_target="tpu_custom_call" | custom-call | bytes 1572864 | tf_op jit(solution)/shard_map/pallas_call | solution.py:203
  2.0 0.0 copy-start
  2.1 0.0 copy-start.2
  2.1 0.0 copy-start.7
  2.1 3.0 %collective-permute-start = (bf16[768,128]{1,0:T(8,128)(2,1)S(1)}, bf16[768,128]{1,0:T(8,128)(2,1)S(1)}, u32[]{:S(2)}, u32[]{:S(2)}) collective-permute-start(bf16[768,128]{1,0:T(8,128)(2,1)S(1)} %get-tuple-element.30), channel_id=1, source_target_pairs={{0,8},{8,0},{16,24},{24,16},{1,9},{9,1},{17,25},{25,17},{2,10},{10... | collective-permute-start | bytes 589832 | tf_op jit(solution)/shard_map/ppermute | solution.py:534
  5.1 1.5 %collective-permute-start.1 = (bf16[768,128]{1,0:T(8,128)(2,1)S(1)}, bf16[768,128]{1,0:T(8,128)(2,1)S(1)}, u32[]{:S(2)}, u32[]{:S(2)}) collective-permute-start(bf16[768,128]{1,0:T(8,128)(2,1)S(1)} %get-tuple-element.31), channel_id=1, source_target_pairs={{0,16},{8,24},{16,0},{24,8},{1,17},{9,25},{17,1},{25,9},{2,18},{10... | collective-permute-start | bytes 589832 | tf_op jit(solution)/shard_map/ppermute | solution.py:534
  6.6 0.0 collective-permute-start.2
  6.7 2.0 %shard_map.138 = (bf16[768,128]{1,0:T(8,128)(2,1)S(1)}, bf16[768,128]{1,0:T(8,128)(2,1)S(1)}, bf16[768,128]{1,0:T(8,128)(2,1)S(1)}, bf16[768,128]{1,0:T(8,128)(2,1)S(1)}) custom-call(s32[8]{0:T(128)} %slots_ref.11, s32[2]{0:T(128)S(1)} %pad_add_fusion.ids_ref, bf16[512,512]{1,0:T(8,128)(2,1)} %q_ref.3, bf16[512,512]{1,0:T(8,128)(2,1)} %k_ref.3, ...), custom_call_target="tpu_custom_call" | custom-call | bytes 1572864 | tf_op jit(solution)/shard_map/pallas_call | solution.py:203
  8.6 2.0 %collective-permute-start.14 = (bf16[768,128]{1,0:T(8,128)(2,1)S(1)}, bf16[768,128]{1,0:T(8,128)(2,1)S(1)}, u32[]{:S(2)}, u32[]{:S(2)}) collective-permute-start(bf16[768,128]{1,0:T(8,128)(2,1)S(1)} %get-tuple-element.39), channel_id=1, source_target_pairs={{0,8},{8,0},{16,24},{24,16},{1,9},{9,1},{17,25},{25,17},{2,10},{10... | collective-permute-start | bytes 589832 | tf_op jit(solution)/shard_map/ppermute | solution.py:534
  10.6 1.5 %collective-permute-start.15 = (bf16[768,128]{1,0:T(8,128)(2,1)S(1)}, bf16[768,128]{1,0:T(8,128)(2,1)S(1)}, u32[]{:S(2)}, u32[]{:S(2)}) collective-permute-start(bf16[768,128]{1,0:T(8,128)(2,1)S(1)} %get-tuple-element.40), channel_id=1, source_target_pairs={{0,16},{8,24},{16,0},{24,8},{1,17},{9,25},{17,1},{25,9},{2,18},{10... | collective-permute-start | bytes 589832 | tf_op jit(solution)/shard_map/ppermute | solution.py:534
  12.2 1.7 %collective-permute-start.16 = (bf16[768,128]{1,0:T(8,128)(2,1)S(1)}, bf16[768,128]{1,0:T(8,128)(2,1)S(1)}, u32[]{:S(2)}, u32[]{:S(2)}) collective-permute-start(bf16[768,128]{1,0:T(8,128)(2,1)S(1)} %get-tuple-element.41), channel_id=1, source_target_pairs={{0,24},{8,16},{16,8},{24,0},{1,25},{9,17},{17,9},{25,1},{2,26},{10... | collective-permute-start | bytes 589832 | tf_op jit(solution)/shard_map/ppermute | solution.py:534
  13.8 2.3 %collective-permute-done.1.refs_2_ = bf16[768,128]{1,0:T(8,128)(2,1)S(1)} collective-permute-done((bf16[768,128]{1,0:T(8,128)(2,1)S(1)}, bf16[768,128]{1,0:T(8,128)(2,1)S(1)}, u32[]{:S(2)}, u32[]{:S(2)}) %collective-permute-start.1) | collective-permute-done | bytes 196640 | tf_op jit(solution)/shard_map/ppermute | solution.py:534
  16.1 0.5 collective-permute-done.2.refs_3_
  16.6 2.3 %attend_low.1 = (bf16[256,128]{1,0:T(8,128)(2,1)S(1)}, bf16[256,128]{1,0:T(8,128)(2,1)S(1)}, bf16[256,128]{1,0:T(8,128)(2,1)S(1)}, bf16[256,128]{1,0:T(8,128)(2,1)S(1)}) custom-call(s32[2]{0:T(128)S(1)} %pad_add_fusion.ids_ref, bf16[768,128]{1,0:T(8,128)(2,1)S(1)} %get-tuple-element.29.refs_0_, bf16[768,128]{1,0:T(8,128)(2,1)S(1)} %collective-permute-done.refs_1_, ...), custom_call_target="tpu_custom_call" | custom-call | flops 335544320 | bytes 1048576 | tf_op jit(solution)/shard_map/attend_low/pallas_call | solution.py:275
  18.9 1.6 %collective-permute-start.3 = (bf16[256,128]{1,0:T(8,128)(2,1)S(1)}, bf16[256,128]{1,0:T(8,128)(2,1)S(1)}, u32[]{:S(2)}, u32[]{:S(2)}) collective-permute-start(bf16[256,128]{1,0:T(8,128)(2,1)S(1)} %get-tuple-element.34), channel_id=1, source_target_pairs={{0,8},{8,0},{16,24},{24,16},{1,9},{9,1},{17,25},{25,17},{2,10},{10... | collective-permute-start | bytes 196616 | tf_op jit(solution)/shard_map/ppermute | solution.py:534
  20.5 0.6 collective-permute-start.4
  21.1 1.5 %collective-permute-start.5 = (bf16[256,128]{1,0:T(8,128)(2,1)S(1)}, bf16[256,128]{1,0:T(8,128)(2,1)S(1)}, u32[]{:S(2)}, u32[]{:S(2)}) collective-permute-start(bf16[256,128]{1,0:T(8,128)(2,1)S(1)} %get-tuple-element.36), channel_id=1, source_target_pairs={{0,24},{8,16},{16,8},{24,0},{1,25},{9,17},{17,9},{25,1},{2,26},{10... | collective-permute-start | bytes 196616 | tf_op jit(solution)/shard_map/ppermute | solution.py:534
  22.5 2.0 %collective-permute-done.15.refs_6_ = bf16[768,128]{1,0:T(8,128)(2,1)S(1)} collective-permute-done((bf16[768,128]{1,0:T(8,128)(2,1)S(1)}, bf16[768,128]{1,0:T(8,128)(2,1)S(1)}, u32[]{:S(2)}, u32[]{:S(2)}) %collective-permute-start.15) | collective-permute-done | bytes 196640 | tf_op jit(solution)/shard_map/ppermute | solution.py:534
  24.6 0.5 collective-permute-done.16.refs_7_
  25.1 3.6 %attend_high.1 = (bf16[256,128]{1,0:T(8,128)(2,1)S(1)}, bf16[256,128]{1,0:T(8,128)(2,1)S(1)}, bf16[256,128]{1,0:T(8,128)(2,1)S(1)}, bf16[256,128]{1,0:T(8,128)(2,1)S(1)}) custom-call(s32[2]{0:T(128)S(1)} %pad_add_fusion.ids_ref, bf16[768,128]{1,0:T(8,128)(2,1)S(1)} %get-tuple-element.29.refs_0_, bf16[768,128]{1,0:T(8,128)(2,1)S(1)} %collective-permute-done.refs_1_, ...), custom_call_target="tpu_custom_call" | custom-call | flops 872415232 | bytes 2097152 | tf_op jit(solution)/shard_map/attend_high/pallas_call | solution.py:275
  28.7 1.5 %collective-permute-start.17 = (bf16[256,128]{1,0:T(8,128)(2,1)S(1)}, bf16[256,128]{1,0:T(8,128)(2,1)S(1)}, u32[]{:S(2)}, u32[]{:S(2)}) collective-permute-start(bf16[256,128]{1,0:T(8,128)(2,1)S(1)} %get-tuple-element.43), channel_id=1, source_target_pairs={{0,8},{8,0},{16,24},{24,16},{1,9},{9,1},{17,25},{25,17},{2,10},{10... | collective-permute-start | bytes 196616 | tf_op jit(solution)/shard_map/ppermute | solution.py:534
  30.2 0.6 collective-permute-start.18
  30.8 1.5 %collective-permute-start.19 = (bf16[256,128]{1,0:T(8,128)(2,1)S(1)}, bf16[256,128]{1,0:T(8,128)(2,1)S(1)}, u32[]{:S(2)}, u32[]{:S(2)}) collective-permute-start(bf16[256,128]{1,0:T(8,128)(2,1)S(1)} %get-tuple-element.45), channel_id=1, source_target_pairs={{0,24},{8,16},{16,8},{24,0},{1,25},{9,17},{17,9},{25,1},{2,26},{10... | collective-permute-start | bytes 196616 | tf_op jit(solution)/shard_map/ppermute | solution.py:534
  32.4 0.1 collective-permute-start.6
  32.5 2.6 %collective-permute-start.9 = (bf16[1024,128]{1,0:T(8,128)(2,1)S(1)}, bf16[1024,128]{1,0:T(8,128)(2,1)S(1)}, u32[]{:S(2)}, u32[]{:S(2)}) collective-permute-start(bf16[1024,128]{1,0:T(8,128)(2,1)S(1)} %constant_dynamic-update-slice_fusion.refs_0_), channel_id=1, source_target_pairs={{0,4},{1,5},{2,6},{3,7},{4,0},{5,1},{6,2},{7,3},{8,12},{9,13},{10,... | collective-permute-start | bytes 786440 | tf_op jit(solution)/shard_map/ppermute | solution.py:492
  35.1 0.7 collective-permute-start.11
  35.9 0.2 collective-permute-done.19
  36.1 2.7 %collective-permute-start.21 = (bf16[1024,128]{1,0:T(8,128)(2,1)S(1)}, bf16[1024,128]{1,0:T(8,128)(2,1)S(1)}, u32[]{:S(2)}, u32[]{:S(2)}) collective-permute-start(bf16[1024,128]{1,0:T(8,128)(2,1)S(1)} %constant_dynamic-update-slice_fusion.4.refs_0_), channel_id=1, source_target_pairs={{0,2},{1,3},{2,0},{3,1},{4,6},{5,7},{6,4},{7,5},{8,10},{9,11},{10,... | collective-permute-start | bytes 786440 | tf_op jit(solution)/shard_map/ppermute | solution.py:492
  38.8 9.5 %collective-permute-done.9.refs_4_ = bf16[1024,128]{1,0:T(8,128)(2,1)S(1)} collective-permute-done((bf16[1024,128]{1,0:T(8,128)(2,1)S(1)}, bf16[1024,128]{1,0:T(8,128)(2,1)S(1)}, u32[]{:S(2)}, u32[]{:S(2)}) %collective-permute-start.9) | collective-permute-done | bytes 262176 | tf_op jit(solution)/shard_map/ppermute | solution.py:492
  48.3 1.3 %collective-permute-start.12 = (bf16[1024,128]{1,0:T(8,128)(2,1)S(1)}, bf16[1024,128]{1,0:T(8,128)(2,1)S(1)}, u32[]{:S(2)}, u32[]{:S(2)}) collective-permute-start(bf16[1024,128]{1,0:T(8,128)(2,1)S(1)} %collective-permute-done.9.refs_4_), channel_id=1, source_target_pairs={{2,0},{3,1},{4,6},{5,7},{10,8},{11,9},{12,14},{13,15},{18,16},{19,... | collective-permute-start | bytes 786440 | tf_op jit(solution)/shard_map/ppermute | solution.py:482
  49.6 2.7 %collective-permute-start.7 = (bf16[1024,128]{1,0:T(8,128)(2,1)S(1)}, bf16[1024,128]{1,0:T(8,128)(2,1)S(1)}, u32[]{:S(2)}, u32[]{:S(2)}) collective-permute-start(bf16[1024,128]{1,0:T(8,128)(2,1)S(1)} %constant_dynamic-update-slice_fusion.refs_0_), channel_id=1, source_target_pairs={{0,2},{1,3},{2,0},{3,1},{4,6},{5,7},{6,4},{7,5},{8,10},{9,11},{10,... | collective-permute-start | bytes 786440 | tf_op jit(solution)/shard_map/ppermute | solution.py:492
  52.3 3.6 %collective-permute-start.23 = (bf16[1024,128]{1,0:T(8,128)(2,1)S(1)}, bf16[1024,128]{1,0:T(8,128)(2,1)S(1)}, u32[]{:S(2)}, u32[]{:S(2)}) collective-permute-start(bf16[1024,128]{1,0:T(8,128)(2,1)S(1)} %constant_dynamic-update-slice_fusion.4.refs_0_), channel_id=1, source_target_pairs={{0,4},{1,5},{2,6},{3,7},{4,0},{5,1},{6,2},{7,3},{8,12},{9,13},{10,... | collective-permute-start | bytes 786440 | tf_op jit(solution)/shard_map/ppermute | solution.py:492
  56.0 0.5 collective-permute-start.25
  56.4 7.3 %collective-permute-done.12 = bf16[1024,128]{1,0:T(8,128)(2,1)S(1)} collective-permute-done((bf16[1024,128]{1,0:T(8,128)(2,1)S(1)}, bf16[1024,128]{1,0:T(8,128)(2,1)S(1)}, u32[]{:S(2)}, u32[]{:S(2)}) %collective-permute-start.12) | collective-permute-done | bytes 262176 | tf_op jit(solution)/shard_map/ppermute | solution.py:482
  63.8 0.1 add.12.refs_6_
  63.8 10.3 %collective-permute-done.7.refs_2_ = bf16[1024,128]{1,0:T(8,128)(2,1)S(1)} collective-permute-done((bf16[1024,128]{1,0:T(8,128)(2,1)S(1)}, bf16[1024,128]{1,0:T(8,128)(2,1)S(1)}, u32[]{:S(2)}, u32[]{:S(2)}) %collective-permute-start.7) | collective-permute-done | bytes 262176 | tf_op jit(solution)/shard_map/ppermute | solution.py:492
  74.1 0.5 collective-permute-start.8
  74.6 0.1 collective-permute-start.13
  74.7 0.4 collective-permute-start.24
  75.1 0.1 collective-permute-start.26
  75.2 1.3 %shard_map.139.base_ref = f32[256,512]{1,0:T(8,128)S(1)} custom-call(s32[8]{0:T(128)S(1)} %copy-done.7, s32[2]{0:T(128)S(1)} %pad_add_fusion.ids_ref, bf16[512,512]{1,0:T(8,128)(2,1)S(1)} %copy-done.2, bf16[4096,512]{1,0:T(8,128)(2,1)S(1)} %copy-done, bf16[1024,128]{1,0:T(8,128)(2,1)S(1)} %constant_dynamic-update-slice_fusion.4.refs_0_, ...), custom_call_target="tpu_custom_call" | custom-call | flops 536870912 | bytes 6291456 | tf_op jit(solution)/shard_map/pallas_call | solution.py:332
  76.6 2.0 %shard_map.137 = (f32[256,512]{1,0:T(8,128)S(1)}, bf16[256,512]{1,0:T(8,128)(2,1)S(1)}, f32[1,256]{1,0:T(1,128)S(1)}) custom-call(s32[8]{0:T(128)S(1)} %copy-done.7, s32[2]{0:T(128)S(1)} %pad_add_fusion.ids_ref, bf16[512,512]{1,0:T(8,128)(2,1)S(1)} %copy-done.2, bf16[4096,512]{1,0:T(8,128)(2,1)S(1)} %copy-done, ...), custom_call_target="tpu_custom_call" | custom-call | flops 1073741824 | bytes 6291456 | tf_op jit(solution)/shard_map/pallas_call | solution.py:332
  78.5 0.0 copy-start.10
  78.5 0.0 copy-start.1
  78.5 0.0 copy-start.4
  78.5 0.0 copy-start.5
  78.6 0.0 copy-start.3
  78.6 0.0 copy-start.6
  78.6 0.0 copy-start.8
  78.6 1.5 %collective-permute-start.30 = (bf16[256,512]{1,0:T(8,128)(2,1)S(1)}, bf16[256,512]{1,0:T(8,128)(2,1)S(1)}, u32[]{:S(2)}, u32[]{:S(2)}) collective-permute-start(bf16[256,512]{1,0:T(8,128)(2,1)S(1)} %get-tuple-element.51), channel_id=1, source_target_pairs={{0,8},{8,16},{16,24},{24,0},{1,9},{9,17},{17,25},{25,1},{2,10},{10... | collective-permute-start | bytes 786440 | tf_op jit(solution)/shard_map/ppermute | solution.py:549
  80.1 2.0 %shard_map.140 = (f32[256,512]{1,0:T(8,128)S(1)}, bf16[256,512]{1,0:T(8,128)(2,1)}, f32[1,512]{1,0:T(1,128)S(1)}) custom-call(s32[8]{0:T(128)S(1)} %copy-done.7, s32[2]{0:T(128)S(1)} %pad_add_fusion.ids_ref, f32[256,512]{1,0:T(8,128)S(1)} %shard_map.139.base_ref, bf16[4096,512]{1,0:T(8,128)(2,1)S(1)} %copy-done, ...), custom_call_target="tpu_custom_call" | custom-call | flops 536870912 | bytes 6291456 | tf_op jit(solution)/shard_map/pallas_call | solution.py:332
  82.1 1.5 %collective-permute-start.31 = (bf16[256,512]{1,0:T(8,128)(2,1)}, bf16[256,512]{1,0:T(8,128)(2,1)S(1)}, u32[]{:S(2)}, u32[]{:S(2)}) collective-permute-start(bf16[256,512]{1,0:T(8,128)(2,1)} %get-tuple-element.52), channel_id=1, source_target_pairs={{0,24},{8,0},{16,8},{24,16},{1,25},{9,1},{17,9},{25,17},{2,26},{10... | collective-permute-start | bytes 786440 | tf_op jit(solution)/shard_map/ppermute | solution.py:558
  83.6 1.2 %collective-permute-done.27 = f32[1,512]{1,0:T(1,128)S(1)} collective-permute-done((f32[1,512]{1,0:T(1,128)S(1)}, f32[1,512]{1,0:T(1,128)S(1)}, u32[]{:S(2)}, u32[]{:S(2)}) %collective-permute-start.27) | collective-permute-done | bytes 2080 | tf_op jit(solution)/shard_map/ppermute | solution.py:503
  84.8 5.3 %collective-permute-start.28 = (f32[1,512]{1,0:T(1,128)S(1)}, f32[1,512]{1,0:T(1,128)S(1)}, u32[]{:S(2)}, u32[]{:S(2)}) collective-permute-start(f32[1,512]{1,0:T(1,128)S(1)} %add.13), channel_id=1, source_target_pairs={{0,2},{1,3},{2,0},{3,1},{4,6},{5,7},{6,4},{7,5},{8,10},{9,11},{10,... | collective-permute-start | bytes 6152 | tf_op jit(solution)/shard_map/ppermute | solution.py:503
  90.1 0.1 copy.15.len_ref
  90.2 1.4 %collective-permute-done.28 = f32[1,512]{1,0:T(1,128)S(1)} collective-permute-done((f32[1,512]{1,0:T(1,128)S(1)}, f32[1,512]{1,0:T(1,128)S(1)}, u32[]{:S(2)}, u32[]{:S(2)}) %collective-permute-start.28) | collective-permute-done | bytes 2080 | tf_op jit(solution)/shard_map/ppermute | solution.py:503
  91.6 3.0 %collective-permute-start.29 = (f32[1,512]{1,0:T(1,128)S(1)}, f32[1,512]{1,0:T(1,128)S(1)}, u32[]{:S(2)}, u32[]{:S(2)}) collective-permute-start(f32[1,512]{1,0:T(1,128)S(1)} %add.14), channel_id=1, source_target_pairs={{0,4},{1,5},{2,6},{3,7},{4,0},{5,1},{6,2},{7,3},{8,12},{9,13},{10,... | collective-permute-start | bytes 6152 | tf_op jit(solution)/shard_map/ppermute | solution.py:503
  94.6 0.5 spectrum.1.spec_ref
  95.2 1.0 collective-permute-done.29
  96.2 0.6 collective-permute-start.32
  96.8 2.8 %collective-permute-start.33 = (f32[1,512]{1,0:T(1,128)S(1)}, f32[1,512]{1,0:T(1,128)S(1)}, u32[]{:S(2)}, u32[]{:S(2)}) collective-permute-start(f32[1,512]{1,0:T(1,128)S(1)} %add.15.sq_ref), channel_id=1, source_target_pairs={{8,16},{16,8},{24,0},{0,24},{9,17},{17,9},{25,1},{1,25},{10,18},{1... | collective-permute-start | bytes 6152 | tf_op jit(solution)/shard_map/ppermute | solution.py:561
  99.6 2.2 %conv_own.1 = (f32[512,512]{1,0:T(8,128)S(1)}, bf16[256,512]{1,0:T(8,128)(2,1)S(1)}) custom-call(f32[256,512]{1,0:T(8,128)S(1)} %get-tuple-element.37.res_low, f32[256,512]{1,0:T(8,128)S(1)} %get-tuple-element.47.res_high, f32[1,512]{1,0:T(1,128)S(1)} %add.15.sq_ref, f32[512,512]{1,0:T(8,128)S(1)} %spectrum.1.spec_ref, f32[1,512]{1,0:T(1,128)S(1)} %bitcast.5, ...), custom_call_target="tpu_custom_call" | custom-call | flops 671088640 | bytes 3145728 | tf_op jit(solution)/shard_map/conv_own/pallas_call | solution.py:563
  101.9 2.7 %conv_last.1 = bf16[512,512]{1,0:T(8,128)(2,1)} custom-call(s32[8]{0:T(128)S(1)} %copy-done.7, s32[2]{0:T(128)S(1)} %pad_add_fusion.ids_ref, f32[512,512]{1,0:T(8,128)S(1)} %get-tuple-element.49.part_ref, bf16[256,512]{1,0:T(8,128)(2,1)S(1)} %get-tuple-element.50.low_ref, bf16[256,512]{1,0:T(8,128)(2,1)S(1)} %collective-permute-done.30.raw_low, ...), custom_call_target="tpu_custom_call" | custom-call | flops 671088640 | bytes 3145728 | tf_op jit(solution)/shard_map/conv_last/pallas_call | solution.py:575
  (50 shorter events, 0.2 us)
Async XLA Ops:
  2.0 73.2 %copy-start = (bf16[4096,512]{1,0:T(8,128)(2,1)S(1)}, bf16[4096,512]{1,0:T(8,128)(2,1)}, u32[]{:S(2)}) copy-start(bf16[4096,512]{1,0:T(8,128)(2,1)} %w_ref.5) | copy-start | bytes 12582916
  2.1 73.2 %copy-start.2 = (bf16[512,512]{1,0:T(8,128)(2,1)S(1)}, bf16[512,512]{1,0:T(8,128)(2,1)}, u32[]{:S(2)}) copy-start(bf16[512,512]{1,0:T(8,128)(2,1)} %base_ref.3) | copy-start | bytes 1572868
  2.1 73.1 %copy-start.7 = (s32[8]{0:T(128)S(1)}, s32[8]{0:T(128)}, u32[]{:S(2)}) copy-start(s32[8]{0:T(128)} %slots_ref.11) | copy-start | bytes 100
  2.1 10.1 %collective-permute-start = (bf16[768,128]{1,0:T(8,128)(2,1)S(1)}, bf16[768,128]{1,0:T(8,128)(2,1)S(1)}, u32[]{:S(2)}, u32[]{:S(2)}) collective-permute-start(bf16[768,128]{1,0:T(8,128)(2,1)S(1)} %get-tuple-element.30), channel_id=1, source_target_pairs={{0,8},{8,0},{16,24},{24,16},{1,9},{9,1},{17,25},{25,17},{2,10},{10... | collective-permute-start | bytes 589832 | tf_op jit(solution)/shard_map/ppermute | solution.py:534
  5.1 11.0 %collective-permute-start.1 = (bf16[768,128]{1,0:T(8,128)(2,1)S(1)}, bf16[768,128]{1,0:T(8,128)(2,1)S(1)}, u32[]{:S(2)}, u32[]{:S(2)}) collective-permute-start(bf16[768,128]{1,0:T(8,128)(2,1)S(1)} %get-tuple-element.31), channel_id=1, source_target_pairs={{0,16},{8,24},{16,0},{24,8},{1,17},{9,25},{17,1},{25,9},{2,18},{10... | collective-permute-start | bytes 589832 | tf_op jit(solution)/shard_map/ppermute | solution.py:534
  6.6 10.0 %collective-permute-start.2 = (bf16[768,128]{1,0:T(8,128)(2,1)S(1)}, bf16[768,128]{1,0:T(8,128)(2,1)S(1)}, u32[]{:S(2)}, u32[]{:S(2)}) collective-permute-start(bf16[768,128]{1,0:T(8,128)(2,1)S(1)} %get-tuple-element.32), channel_id=1, source_target_pairs={{0,24},{8,16},{16,8},{24,0},{1,25},{9,17},{17,9},{25,1},{2,26},{10... | collective-permute-start | bytes 589832 | tf_op jit(solution)/shard_map/ppermute | solution.py:534
  8.6 12.5 %collective-permute-start.14 = (bf16[768,128]{1,0:T(8,128)(2,1)S(1)}, bf16[768,128]{1,0:T(8,128)(2,1)S(1)}, u32[]{:S(2)}, u32[]{:S(2)}) collective-permute-start(bf16[768,128]{1,0:T(8,128)(2,1)S(1)} %get-tuple-element.39), channel_id=1, source_target_pairs={{0,8},{8,0},{16,24},{24,16},{1,9},{9,1},{17,25},{25,17},{2,10},{10... | collective-permute-start | bytes 589832 | tf_op jit(solution)/shard_map/ppermute | solution.py:534
  10.6 13.9 %collective-permute-start.15 = (bf16[768,128]{1,0:T(8,128)(2,1)S(1)}, bf16[768,128]{1,0:T(8,128)(2,1)S(1)}, u32[]{:S(2)}, u32[]{:S(2)}) collective-permute-start(bf16[768,128]{1,0:T(8,128)(2,1)S(1)} %get-tuple-element.40), channel_id=1, source_target_pairs={{0,16},{8,24},{16,0},{24,8},{1,17},{9,25},{17,1},{25,9},{2,18},{10... | collective-permute-start | bytes 589832 | tf_op jit(solution)/shard_map/ppermute | solution.py:534
  12.2 12.9 %collective-permute-start.16 = (bf16[768,128]{1,0:T(8,128)(2,1)S(1)}, bf16[768,128]{1,0:T(8,128)(2,1)S(1)}, u32[]{:S(2)}, u32[]{:S(2)}) collective-permute-start(bf16[768,128]{1,0:T(8,128)(2,1)S(1)} %get-tuple-element.41), channel_id=1, source_target_pairs={{0,24},{8,16},{16,8},{24,0},{1,25},{9,17},{17,9},{25,1},{2,26},{10... | collective-permute-start | bytes 589832 | tf_op jit(solution)/shard_map/ppermute | solution.py:534
  18.9 11.9 %collective-permute-start.3 = (bf16[256,128]{1,0:T(8,128)(2,1)S(1)}, bf16[256,128]{1,0:T(8,128)(2,1)S(1)}, u32[]{:S(2)}, u32[]{:S(2)}) collective-permute-start(bf16[256,128]{1,0:T(8,128)(2,1)S(1)} %get-tuple-element.34), channel_id=1, source_target_pairs={{0,8},{8,0},{16,24},{24,16},{1,9},{9,1},{17,25},{25,17},{2,10},{10... | collective-permute-start | bytes 196616 | tf_op jit(solution)/shard_map/ppermute | solution.py:534
  20.5 11.9 %collective-permute-start.4 = (bf16[256,128]{1,0:T(8,128)(2,1)S(1)}, bf16[256,128]{1,0:T(8,128)(2,1)S(1)}, u32[]{:S(2)}, u32[]{:S(2)}) collective-permute-start(bf16[256,128]{1,0:T(8,128)(2,1)S(1)} %get-tuple-element.35), channel_id=1, source_target_pairs={{0,16},{8,24},{16,0},{24,8},{1,17},{9,25},{17,1},{25,9},{2,18},{10... | collective-permute-start | bytes 196616 | tf_op jit(solution)/shard_map/ppermute | solution.py:534
  21.1 11.3 %collective-permute-start.5 = (bf16[256,128]{1,0:T(8,128)(2,1)S(1)}, bf16[256,128]{1,0:T(8,128)(2,1)S(1)}, u32[]{:S(2)}, u32[]{:S(2)}) collective-permute-start(bf16[256,128]{1,0:T(8,128)(2,1)S(1)} %get-tuple-element.36), channel_id=1, source_target_pairs={{0,24},{8,16},{16,8},{24,0},{1,25},{9,17},{17,9},{25,1},{2,26},{10... | collective-permute-start | bytes 196616 | tf_op jit(solution)/shard_map/ppermute | solution.py:534
  28.7 6.4 %collective-permute-start.17 = (bf16[256,128]{1,0:T(8,128)(2,1)S(1)}, bf16[256,128]{1,0:T(8,128)(2,1)S(1)}, u32[]{:S(2)}, u32[]{:S(2)}) collective-permute-start(bf16[256,128]{1,0:T(8,128)(2,1)S(1)} %get-tuple-element.43), channel_id=1, source_target_pairs={{0,8},{8,0},{16,24},{24,16},{1,9},{9,1},{17,25},{25,17},{2,10},{10... | collective-permute-start | bytes 196616 | tf_op jit(solution)/shard_map/ppermute | solution.py:534
  30.2 5.6 %collective-permute-start.18 = (bf16[256,128]{1,0:T(8,128)(2,1)S(1)}, bf16[256,128]{1,0:T(8,128)(2,1)S(1)}, u32[]{:S(2)}, u32[]{:S(2)}) collective-permute-start(bf16[256,128]{1,0:T(8,128)(2,1)S(1)} %get-tuple-element.44), channel_id=1, source_target_pairs={{0,16},{8,24},{16,0},{24,8},{1,17},{9,25},{17,1},{25,9},{2,18},{10... | collective-permute-start | bytes 196616 | tf_op jit(solution)/shard_map/ppermute | solution.py:534
  30.8 5.2 %collective-permute-start.19 = (bf16[256,128]{1,0:T(8,128)(2,1)S(1)}, bf16[256,128]{1,0:T(8,128)(2,1)S(1)}, u32[]{:S(2)}, u32[]{:S(2)}) collective-permute-start(bf16[256,128]{1,0:T(8,128)(2,1)S(1)} %get-tuple-element.45), channel_id=1, source_target_pairs={{0,24},{8,16},{16,8},{24,0},{1,25},{9,17},{17,9},{25,1},{2,26},{10... | collective-permute-start | bytes 196616 | tf_op jit(solution)/shard_map/ppermute | solution.py:534
  32.4 19.9 %collective-permute-start.6 = (bf16[1024,128]{1,0:T(8,128)(2,1)S(1)}, bf16[1024,128]{1,0:T(8,128)(2,1)S(1)}, u32[]{:S(2)}, u32[]{:S(2)}) collective-permute-start(bf16[1024,128]{1,0:T(8,128)(2,1)S(1)} %constant_dynamic-update-slice_fusion.refs_0_), channel_id=1, source_target_pairs={{0,1},{1,0},{2,3},{3,2},{4,5},{5,4},{6,7},{7,6},{8,9},{9,8},{10,11... | collective-permute-start | bytes 786440 | tf_op jit(solution)/shard_map/ppermute | solution.py:496
  32.5 15.8 %collective-permute-start.9 = (bf16[1024,128]{1,0:T(8,128)(2,1)S(1)}, bf16[1024,128]{1,0:T(8,128)(2,1)S(1)}, u32[]{:S(2)}, u32[]{:S(2)}) collective-permute-start(bf16[1024,128]{1,0:T(8,128)(2,1)S(1)} %constant_dynamic-update-slice_fusion.refs_0_), channel_id=1, source_target_pairs={{0,4},{1,5},{2,6},{3,7},{4,0},{5,1},{6,2},{7,3},{8,12},{9,13},{10,... | collective-permute-start | bytes 786440 | tf_op jit(solution)/shard_map/ppermute | solution.py:492
  35.1 17.2 %collective-permute-start.11 = (bf16[1024,128]{1,0:T(8,128)(2,1)S(1)}, bf16[1024,128]{1,0:T(8,128)(2,1)S(1)}, u32[]{:S(2)}, u32[]{:S(2)}) collective-permute-start(bf16[1024,128]{1,0:T(8,128)(2,1)S(1)} %constant_dynamic-update-slice_fusion.refs_0_), channel_id=1, source_target_pairs={{2,4},{3,5},{4,2},{5,3},{10,12},{11,13},{12,10},{13,11},{18,20},{1... | collective-permute-start | bytes 786440 | tf_op jit(solution)/shard_map/ppermute | solution.py:480
  36.1 19.9 %collective-permute-start.21 = (bf16[1024,128]{1,0:T(8,128)(2,1)S(1)}, bf16[1024,128]{1,0:T(8,128)(2,1)S(1)}, u32[]{:S(2)}, u32[]{:S(2)}) collective-permute-start(bf16[1024,128]{1,0:T(8,128)(2,1)S(1)} %constant_dynamic-update-slice_fusion.4.refs_0_), channel_id=1, source_target_pairs={{0,2},{1,3},{2,0},{3,1},{4,6},{5,7},{6,4},{7,5},{8,10},{9,11},{10,... | collective-permute-start | bytes 786440 | tf_op jit(solution)/shard_map/ppermute | solution.py:492
  48.3 15.5 %collective-permute-start.12 = (bf16[1024,128]{1,0:T(8,128)(2,1)S(1)}, bf16[1024,128]{1,0:T(8,128)(2,1)S(1)}, u32[]{:S(2)}, u32[]{:S(2)}) collective-permute-start(bf16[1024,128]{1,0:T(8,128)(2,1)S(1)} %collective-permute-done.9.refs_4_), channel_id=1, source_target_pairs={{2,0},{3,1},{4,6},{5,7},{10,8},{11,9},{12,14},{13,15},{18,16},{19,... | collective-permute-start | bytes 786440 | tf_op jit(solution)/shard_map/ppermute | solution.py:482
  49.6 24.5 %collective-permute-start.7 = (bf16[1024,128]{1,0:T(8,128)(2,1)S(1)}, bf16[1024,128]{1,0:T(8,128)(2,1)S(1)}, u32[]{:S(2)}, u32[]{:S(2)}) collective-permute-start(bf16[1024,128]{1,0:T(8,128)(2,1)S(1)} %constant_dynamic-update-slice_fusion.refs_0_), channel_id=1, source_target_pairs={{0,2},{1,3},{2,0},{3,1},{4,6},{5,7},{6,4},{7,5},{8,10},{9,11},{10,... | collective-permute-start | bytes 786440 | tf_op jit(solution)/shard_map/ppermute | solution.py:492
  52.3 21.8 %collective-permute-start.20 = (bf16[1024,128]{1,0:T(8,128)(2,1)S(1)}, bf16[1024,128]{1,0:T(8,128)(2,1)S(1)}, u32[]{:S(2)}, u32[]{:S(2)}) collective-permute-start(bf16[1024,128]{1,0:T(8,128)(2,1)S(1)} %constant_dynamic-update-slice_fusion.4.refs_0_), channel_id=1, source_target_pairs={{0,1},{1,0},{2,3},{3,2},{4,5},{5,4},{6,7},{7,6},{8,9},{9,8},{10,11... | collective-permute-start | bytes 786440 | tf_op jit(solution)/shard_map/ppermute | solution.py:496
  52.3 22.3 %collective-permute-start.23 = (bf16[1024,128]{1,0:T(8,128)(2,1)S(1)}, bf16[1024,128]{1,0:T(8,128)(2,1)S(1)}, u32[]{:S(2)}, u32[]{:S(2)}) collective-permute-start(bf16[1024,128]{1,0:T(8,128)(2,1)S(1)} %constant_dynamic-update-slice_fusion.4.refs_0_), channel_id=1, source_target_pairs={{0,4},{1,5},{2,6},{3,7},{4,0},{5,1},{6,2},{7,3},{8,12},{9,13},{10,... | collective-permute-start | bytes 786440 | tf_op jit(solution)/shard_map/ppermute | solution.py:492
  56.0 18.7 %collective-permute-start.25 = (bf16[1024,128]{1,0:T(8,128)(2,1)S(1)}, bf16[1024,128]{1,0:T(8,128)(2,1)S(1)}, u32[]{:S(2)}, u32[]{:S(2)}) collective-permute-start(bf16[1024,128]{1,0:T(8,128)(2,1)S(1)} %constant_dynamic-update-slice_fusion.4.refs_0_), channel_id=1, source_target_pairs={{0,6},{1,7},{2,4},{3,5},{4,2},{5,3},{6,0},{7,1},{8,14},{9,15},{10,... | collective-permute-start | bytes 786440 | tf_op jit(solution)/shard_map/ppermute | solution.py:492
  63.7 11.4 %collective-permute-start.22 = (bf16[1024,128]{1,0:T(8,128)(2,1)S(1)}, bf16[1024,128]{1,0:T(8,128)(2,1)S(1)}, u32[]{:S(2)}, u32[]{:S(2)}) collective-permute-start(bf16[1024,128]{1,0:T(8,128)(2,1)S(1)} %collective-permute-done.21.refs_2_), channel_id=1, source_target_pairs={{0,1},{1,0},{2,3},{3,2},{4,5},{5,4},{6,7},{7,6},{8,9},{9,8},{10,11... | collective-permute-start | bytes 786440 | tf_op jit(solution)/shard_map/ppermute | solution.py:496
  74.1 2.4 %collective-permute-start.10 = (bf16[1024,128]{1,0:T(8,128)(2,1)S(1)}, bf16[1024,128]{1,0:T(8,128)(2,1)S(1)}, u32[]{:S(2)}, u32[]{:S(2)}) collective-permute-start(bf16[1024,128]{1,0:T(8,128)(2,1)S(1)} %collective-permute-done.9.refs_4_), channel_id=1, source_target_pairs={{0,1},{1,0},{2,3},{3,2},{4,5},{5,4},{6,7},{7,6},{8,9},{9,8},{10,11... | collective-permute-start | bytes 786440 | tf_op jit(solution)/shard_map/ppermute | solution.py:496
  74.1 2.4 %collective-permute-start.8 = (bf16[1024,128]{1,0:T(8,128)(2,1)S(1)}, bf16[1024,128]{1,0:T(8,128)(2,1)S(1)}, u32[]{:S(2)}, u32[]{:S(2)}) collective-permute-start(bf16[1024,128]{1,0:T(8,128)(2,1)S(1)} %collective-permute-done.7.refs_2_), channel_id=1, source_target_pairs={{0,1},{1,0},{2,3},{3,2},{4,5},{5,4},{6,7},{7,6},{8,9},{9,8},{10,11... | collective-permute-start | bytes 786440 | tf_op jit(solution)/shard_map/ppermute | solution.py:496
  74.6 1.9 %collective-permute-start.13 = (bf16[1024,128]{1,0:T(8,128)(2,1)S(1)}, bf16[1024,128]{1,0:T(8,128)(2,1)S(1)}, u32[]{:S(2)}, u32[]{:S(2)}) collective-permute-start(bf16[1024,128]{1,0:T(8,128)(2,1)S(1)} %add.12.refs_6_), channel_id=1, source_target_pairs={{0,1},{1,0},{2,3},{3,2},{4,5},{5,4},{6,7},{7,6},{8,9},{9,8},{10,11... | collective-permute-start | bytes 786440 | tf_op jit(solution)/shard_map/ppermute | solution.py:496
  74.7 5.4 %collective-permute-start.24 = (bf16[1024,128]{1,0:T(8,128)(2,1)S(1)}, bf16[1024,128]{1,0:T(8,128)(2,1)S(1)}, u32[]{:S(2)}, u32[]{:S(2)}) collective-permute-start(bf16[1024,128]{1,0:T(8,128)(2,1)S(1)} %collective-permute-done.23.refs_0_), channel_id=1, source_target_pairs={{0,1},{1,0},{2,3},{3,2},{4,5},{5,4},{6,7},{7,6},{8,9},{9,8},{10,11... | collective-permute-start | bytes 786440 | tf_op jit(solution)/shard_map/ppermute | solution.py:496
  75.1 5.0 %collective-permute-start.26 = (bf16[1024,128]{1,0:T(8,128)(2,1)S(1)}, bf16[1024,128]{1,0:T(8,128)(2,1)S(1)}, u32[]{:S(2)}, u32[]{:S(2)}) collective-permute-start(bf16[1024,128]{1,0:T(8,128)(2,1)S(1)} %collective-permute-done.25.refs_2_), channel_id=1, source_target_pairs={{0,1},{1,0},{2,3},{3,2},{4,5},{5,4},{6,7},{7,6},{8,9},{9,8},{10,11... | collective-permute-start | bytes 786440 | tf_op jit(solution)/shard_map/ppermute | solution.py:496
  78.5 11.6 %copy-start.10 = (s32[512]{0:T(512)S(1)}, s32[512]{0:T(512)}, u32[]{:S(2)}) copy-start(s32[512]{0:T(512)} %param.21) | copy-start | bytes 6148
  78.5 16.1 %copy-start.1 = (bf16[512,256]{1,0:T(8,128)(2,1)S(1)}, bf16[512,256]{1,0:T(8,128)(2,1)}, u32[]{:S(2)}) copy-start(bf16[512,256]{1,0:T(8,128)(2,1)} %constant.16.clone.fh_ref.fh) | copy-start | bytes 786436
  78.5 16.1 %copy-start.4 = (bf16[512,256]{1,0:T(8,128)(2,1)S(1)}, bf16[512,256]{1,0:T(8,128)(2,1)}, u32[]{:S(2)}) copy-start(bf16[512,256]{1,0:T(8,128)(2,1)} %constant.17.clone.fl_ref.fl) | copy-start | bytes 786436
  78.5 16.1 %copy-start.5 = (bf16[512,256]{1,0:T(8,128)(2,1)S(1)}, bf16[512,256]{1,0:T(8,128)(2,1)}, u32[]{:S(2)}) copy-start(bf16[512,256]{1,0:T(8,128)(2,1)} %filters_ref.1) | copy-start | bytes 786436
  78.6 21.1 %copy-start.3 = (bf16[256,512]{1,0:T(8,128)(2,1)S(1)}, bf16[256,512]{1,0:T(8,128)(2,1)}, u32[]{:S(2)}) copy-start(bf16[256,512]{1,0:T(8,128)(2,1)} %constant.18.clone.gh) | copy-start | bytes 786436
  78.6 21.1 %copy-start.6 = (bf16[256,512]{1,0:T(8,128)(2,1)S(1)}, bf16[256,512]{1,0:T(8,128)(2,1)}, u32[]{:S(2)}) copy-start(bf16[256,512]{1,0:T(8,128)(2,1)} %constant.19.clone.gl) | copy-start | bytes 786436
  78.6 21.1 %copy-start.8 = (f32[512]{0:T(512)S(1)}, f32[512]{0:T(512)}, u32[]{:S(2)}) copy-start(f32[512]{0:T(512)} %param.19) | copy-start | bytes 6148
  78.6 21.0 %copy-start.9 = (f32[512]{0:T(512)S(1)}, f32[512]{0:T(512)}, u32[]{:S(2)}) copy-start(f32[512]{0:T(512)} %param.22) | copy-start | bytes 6148
  78.6 23.2 %collective-permute-start.30 = (bf16[256,512]{1,0:T(8,128)(2,1)S(1)}, bf16[256,512]{1,0:T(8,128)(2,1)S(1)}, u32[]{:S(2)}, u32[]{:S(2)}) collective-permute-start(bf16[256,512]{1,0:T(8,128)(2,1)S(1)} %get-tuple-element.51), channel_id=1, source_target_pairs={{0,8},{8,16},{16,24},{24,0},{1,9},{9,17},{17,25},{25,1},{2,10},{10... | collective-permute-start | bytes 786440 | tf_op jit(solution)/shard_map/ppermute | solution.py:549
  82.1 19.7 %collective-permute-start.31 = (bf16[256,512]{1,0:T(8,128)(2,1)}, bf16[256,512]{1,0:T(8,128)(2,1)S(1)}, u32[]{:S(2)}, u32[]{:S(2)}) collective-permute-start(bf16[256,512]{1,0:T(8,128)(2,1)} %get-tuple-element.52), channel_id=1, source_target_pairs={{0,24},{8,0},{16,8},{24,16},{1,25},{9,1},{17,9},{25,17},{2,26},{10... | collective-permute-start | bytes 786440 | tf_op jit(solution)/shard_map/ppermute | solution.py:558
  83.6 1.2 %collective-permute-start.27 = (f32[1,512]{1,0:T(1,128)S(1)}, f32[1,512]{1,0:T(1,128)S(1)}, u32[]{:S(2)}, u32[]{:S(2)}) collective-permute-start(f32[1,512]{1,0:T(1,128)S(1)} %get-tuple-element.48), channel_id=1, source_target_pairs={{0,1},{1,0},{2,3},{3,2},{4,5},{5,4},{6,7},{7,6},{8,9},{9,8},{10,11... | collective-permute-start | bytes 6152 | tf_op jit(solution)/shard_map/ppermute | solution.py:503
  84.8 6.9 %collective-permute-start.28 = (f32[1,512]{1,0:T(1,128)S(1)}, f32[1,512]{1,0:T(1,128)S(1)}, u32[]{:S(2)}, u32[]{:S(2)}) collective-permute-start(f32[1,512]{1,0:T(1,128)S(1)} %add.13), channel_id=1, source_target_pairs={{0,2},{1,3},{2,0},{3,1},{4,6},{5,7},{6,4},{7,5},{8,10},{9,11},{10,... | collective-permute-start | bytes 6152 | tf_op jit(solution)/shard_map/ppermute | solution.py:503
  91.6 4.6 %collective-permute-start.29 = (f32[1,512]{1,0:T(1,128)S(1)}, f32[1,512]{1,0:T(1,128)S(1)}, u32[]{:S(2)}, u32[]{:S(2)}) collective-permute-start(f32[1,512]{1,0:T(1,128)S(1)} %add.14), channel_id=1, source_target_pairs={{0,4},{1,5},{2,6},{3,7},{4,0},{5,1},{6,2},{7,3},{8,12},{9,13},{10,... | collective-permute-start | bytes 6152 | tf_op jit(solution)/shard_map/ppermute | solution.py:503
  96.2 5.6 %collective-permute-start.32 = (f32[1,512]{1,0:T(1,128)S(1)}, f32[1,512]{1,0:T(1,128)S(1)}, u32[]{:S(2)}, u32[]{:S(2)}) collective-permute-start(f32[1,512]{1,0:T(1,128)S(1)} %add.15.sq_ref), channel_id=1, source_target_pairs={{0,8},{8,0},{16,24},{24,16},{1,9},{9,1},{17,25},{25,17},{2,10},{10... | collective-permute-start | bytes 6152 | tf_op jit(solution)/shard_map/ppermute | solution.py:560
  96.8 5.0 %collective-permute-start.33 = (f32[1,512]{1,0:T(1,128)S(1)}, f32[1,512]{1,0:T(1,128)S(1)}, u32[]{:S(2)}, u32[]{:S(2)}) collective-permute-start(f32[1,512]{1,0:T(1,128)S(1)} %add.15.sq_ref), channel_id=1, source_target_pairs={{8,16},{16,8},{24,0},{0,24},{9,17},{17,9},{25,1},{1,25},{10,18},{1... | collective-permute-start | bytes 6152 | tf_op jit(solution)/shard_map/ppermute | solution.py:561
where the time goes:
time: 105 us
  starting transfers between devices  47 us (45%)
  waiting for transfers between devices  36.3 us (35%)
  Pallas kernels  20.4 us (19%)
    ppermute x5, waiting for transfers between devices, gather_mp(): pieces.append(lax.ppermute(own, 'mp', xor_route(size, 2 * k)))  19.8 us
    ppermute x12, starting transfers between devices, exchange(): lax.ppermute(pieces[k], 'seq', xor_route(n, k))  17 us
    ppermute x5, starting transfers between devices, gather_mp(): pieces.append(lax.ppermute(own, 'mp', xor_route(size, 2 * k)))  12.2 us
    ppermute x3, starting transfers between devices, total_mp(): part = part + lax.ppermute(part, 'mp', xor_route(size, k))  8.3 us
    ppermute x1, waiting for transfers between devices, relayed_piece(): return direct + lax.ppermute(near, 'mp', ends)  7.33 us
    pallas_call x2, Pallas kernels, attend(): pl.pallas_call(functools.partial(attend_kernel, n, high, rows), out_shape...  5.91 us
    ppermute x12, waiting for transfers between devices, exchange(): lax.ppermute(pieces[k], 'seq', xor_route(n, k))  5.52 us
    pallas_call x3, Pallas kernels, project(): pl.pallas_call(functools.partial(project_kernel, n, high, indices, len(ex...  5.26 us
  transfers between devices with their start and end apart: 34, of which 11 were waited for; matrix products, arithmetic and copies ran while one was open for 0% of the time, Pallas kernels for 15%

commit v1 on v0

--- a/solution.py
+++ b/solution.py
@@ -490,6 +490,10 @@
             pieces.append(relayed_piece(own, pieces[k - 1], size))
         else:
             pieces.append(lax.ppermute(own, "mp", xor_route(size, 2 * k)))
+    return pieces
+
+
+def with_sibling(pieces, size):
     parts = []
     for piece in pieces:
         parts.append(piece)
@@ -539,9 +543,13 @@
     spec = spectrum(filters, filter_len, forward)
 
     att_low = exchange(attend(n, 0, rows, ids, low))
-    parts_low = gather_mp(jnp.concatenate(att_low, axis=0), mp_size, True)
+    early = gather_mp(att_low[0], mp_size, False)
+    late = gather_mp(jnp.concatenate(att_low[1:], axis=0), mp_size, True)
+    parts_low = with_sibling([jnp.concatenate(p, axis=0) for p in zip(early, late)], mp_size)
     att_high = exchange(attend(n, 1, rows, ids, low + high))
-    parts_high = gather_mp(jnp.concatenate(att_high, axis=0), mp_size, False)
+    early = gather_mp(att_high[0], mp_size, False)
+    late = gather_mp(jnp.concatenate(att_high[1:], axis=0), mp_size, False)
+    parts_high = with_sibling([jnp.concatenate(p, axis=0) for p in zip(early, late)], mp_size)
 
     most = mp_size // 2
     every = tuple(range(mp_size))

time: 105 us -> 112 us (1.067)
  waiting for transfers between devices: 36.3 us -> 41.5 us
  starting transfers between devices: 47 us -> 49.1 us
    ppermute x12, waiting for transfers between devices: 5.52 us -> 19.1 us  [exchange(): lax.ppermute(pieces[k], 'seq', xor_route(n, k))]
    ppermute x1, waiting for transfers between devices: 7.33 us -> 0.42 us  [relayed_piece(): return direct + lax.ppermute(near, 'mp', ends)]
    ppermute x5 -> x11, starting transfers between devices: 12.2 us -> 17.4 us  [gather_mp(): pieces.append(lax.ppermute(own, 'mp', xor_route(size, 2 * k)))]
    ppermute x3, starting transfers between devices: 8.3 us -> 4.49 us  [total_mp(): part = part + lax.ppermute(part, 'mp', xor_route(size, k))]
    ppermute x5 -> x11, waiting for transfers between devices: 19.8 us -> 16.7 us  [gather_mp(): pieces.append(lax.ppermute(own, 'mp', xor_route(size, 2 * k)))]
    ppermute x12, starting transfers between devices: 17 us -> 18.8 us  [exchange(): lax.ppermute(pieces[k], 'seq', xor_route(n, k))]
    ppermute x1, starting transfers between devices: 2.83 us -> 1.29 us  [fast_device(): sq_b = lax.ppermute(squares, 'seq', pairs(n, 1))]
  transfers between devices with their start and end apart: 34 -> 40, of which waited for: 11 -> 16; matrix products, arithmetic and copies ran while one was open for 0% -> 0% of each run, Pallas kernels for 15% -> 14%
where the time goes in v1:
time: 112 us
  starting transfers between devices  49.1 us (44%)
  waiting for transfers between devices  41.5 us (37%)
  Pallas kernels  20.5 us (18%)
    ppermute x12, waiting for transfers between devices, exchange(): lax.ppermute(pieces[k], 'seq', xor_route(n, k))  19.1 us
    ppermute x12, starting transfers between devices, exchange(): lax.ppermute(pieces[k], 'seq', xor_route(n, k))  18.8 us
    ppermute x11, starting transfers between devices, gather_mp(): pieces.append(lax.ppermute(own, 'mp', xor_route(size, 2 * k)))  17.4 us
    ppermute x11, waiting for transfers between devices, gather_mp(): pieces.append(lax.ppermute(own, 'mp', xor_route(size, 2 * k)))  16.7 us
    pallas_call x2, Pallas kernels, attend(): pl.pallas_call(functools.partial(attend_kernel, n, high, rows), out_shape...  5.91 us
    pallas_call x3, Pallas kernels, project(): pl.pallas_call(functools.partial(project_kernel, n, high, indices, len(ex...  5.27 us
    ppermute x3, starting transfers between devices, total_mp(): part = part + lax.ppermute(part, 'mp', xor_route(size, k))  4.49 us
    ppermute x3, waiting for transfers between devices, total_mp(): part = part + lax.ppermute(part, 'mp', xor_route(size, k))  4.28 us
  transfers between devices with their start and end apart: 40, of which 16 were waited for; matrix products, arithmetic and copies ran while one was open for 0% of the time, Pallas kernels for 14%

profile of v1, /device:TPU:0, one launch (start us, length us, event | category | flops | bytes accessed | tf_op | source)
XLA Modules:
  0.0 112.2 jit_solution(5960681973390797449)
XLA Ops:
  0.0 0.1 pad_add_fusion.ids_ref
  0.1 2.0 %shard_map.136 = (bf16[768,128]{1,0:T(8,128)(2,1)S(1)}, bf16[768,128]{1,0:T(8,128)(2,1)S(1)}, bf16[768,128]{1,0:T(8,128)(2,1)S(1)}, bf16[768,128]{1,0:T(8,128)(2,1)S(1)}) custom-call(s32[8]{0:T(128)} %slots_ref.11, s32[2]{0:T(128)S(1)} %pad_add_fusion.ids_ref, bf16[512,512]{1,0:T(8,128)(2,1)} %q_ref.3, bf16[512,512]{1,0:T(8,128)(2,1)} %k_ref.3, ...), custom_call_target="tpu_custom_call" | custom-call | bytes 1572864 | tf_op jit(solution)/shard_map/pallas_call | solution.py:203
  2.0 3.0 %collective-permute-start = (bf16[768,128]{1,0:T(8,128)(2,1)S(1)}, bf16[768,128]{1,0:T(8,128)(2,1)S(1)}, u32[]{:S(2)}, u32[]{:S(2)}) collective-permute-start(bf16[768,128]{1,0:T(8,128)(2,1)S(1)} %get-tuple-element.30), channel_id=1, source_target_pairs={{0,8},{8,0},{16,24},{24,16},{1,9},{9,1},{17,25},{25,17},{2,10},{10... | collective-permute-start | bytes 589832 | tf_op jit(solution)/shard_map/ppermute | solution.py:538
  5.1 1.5 %collective-permute-start.1 = (bf16[768,128]{1,0:T(8,128)(2,1)S(1)}, bf16[768,128]{1,0:T(8,128)(2,1)S(1)}, u32[]{:S(2)}, u32[]{:S(2)}) collective-permute-start(bf16[768,128]{1,0:T(8,128)(2,1)S(1)} %get-tuple-element.31), channel_id=1, source_target_pairs={{0,16},{8,24},{16,0},{24,8},{1,17},{9,25},{17,1},{25,9},{2,18},{10... | collective-permute-start | bytes 589832 | tf_op jit(solution)/shard_map/ppermute | solution.py:538
  6.6 2.0 %shard_map.138 = (bf16[768,128]{1,0:T(8,128)(2,1)S(1)}, bf16[768,128]{1,0:T(8,128)(2,1)S(1)}, bf16[768,128]{1,0:T(8,128)(2,1)S(1)}, bf16[768,128]{1,0:T(8,128)(2,1)S(1)}) custom-call(s32[8]{0:T(128)} %slots_ref.11, s32[2]{0:T(128)S(1)} %pad_add_fusion.ids_ref, bf16[512,512]{1,0:T(8,128)(2,1)} %q_ref.3, bf16[512,512]{1,0:T(8,128)(2,1)} %k_ref.3, ...), custom_call_target="tpu_custom_call" | custom-call | bytes 1572864 | tf_op jit(solution)/shard_map/pallas_call | solution.py:203
  8.6 2.0 %collective-permute-start.17 = (bf16[768,128]{1,0:T(8,128)(2,1)S(1)}, bf16[768,128]{1,0:T(8,128)(2,1)S(1)}, u32[]{:S(2)}, u32[]{:S(2)}) collective-permute-start(bf16[768,128]{1,0:T(8,128)(2,1)S(1)} %get-tuple-element.39), channel_id=1, source_target_pairs={{0,8},{8,0},{16,24},{24,16},{1,9},{9,1},{17,25},{25,17},{2,10},{10... | collective-permute-start | bytes 589832 | tf_op jit(solution)/shard_map/ppermute | solution.py:538
  10.6 1.5 %collective-permute-start.18 = (bf16[768,128]{1,0:T(8,128)(2,1)S(1)}, bf16[768,128]{1,0:T(8,128)(2,1)S(1)}, u32[]{:S(2)}, u32[]{:S(2)}) collective-permute-start(bf16[768,128]{1,0:T(8,128)(2,1)S(1)} %get-tuple-element.40), channel_id=1, source_target_pairs={{0,16},{8,24},{16,0},{24,8},{1,17},{9,25},{17,1},{25,9},{2,18},{10... | collective-permute-start | bytes 589832 | tf_op jit(solution)/shard_map/ppermute | solution.py:538
  12.1 1.7 %collective-permute-start.19 = (bf16[768,128]{1,0:T(8,128)(2,1)S(1)}, bf16[768,128]{1,0:T(8,128)(2,1)S(1)}, u32[]{:S(2)}, u32[]{:S(2)}) collective-permute-start(bf16[768,128]{1,0:T(8,128)(2,1)S(1)} %get-tuple-element.41), channel_id=1, source_target_pairs={{0,24},{8,16},{16,8},{24,0},{1,25},{9,17},{17,9},{25,1},{2,26},{10... | collective-permute-start | bytes 589832 | tf_op jit(solution)/shard_map/ppermute | solution.py:538
  13.8 2.3 %collective-permute-done.1.refs_2_ = bf16[768,128]{1,0:T(8,128)(2,1)S(1)} collective-permute-done((bf16[768,128]{1,0:T(8,128)(2,1)S(1)}, bf16[768,128]{1,0:T(8,128)(2,1)S(1)}, u32[]{:S(2)}, u32[]{:S(2)}) %collective-permute-start.1) | collective-permute-done | bytes 196640 | tf_op jit(solution)/shard_map/ppermute | solution.py:538
  16.1 0.5 collective-permute-done.2.refs_3_
  16.6 2.3 %attend_low.1 = (bf16[256,128]{1,0:T(8,128)(2,1)S(1)}, bf16[256,128]{1,0:T(8,128)(2,1)S(1)}, bf16[256,128]{1,0:T(8,128)(2,1)S(1)}, bf16[256,128]{1,0:T(8,128)(2,1)S(1)}) custom-call(s32[2]{0:T(128)S(1)} %pad_add_fusion.ids_ref, bf16[768,128]{1,0:T(8,128)(2,1)S(1)} %get-tuple-element.29.refs_0_, bf16[768,128]{1,0:T(8,128)(2,1)S(1)} %collective-permute-done.refs_1_, ...), custom_call_target="tpu_custom_call" | custom-call | flops 335544320 | bytes 1048576 | tf_op jit(solution)/shard_map/attend_low/pallas_call | solution.py:275
  18.9 1.6 %collective-permute-start.7 = (bf16[256,128]{1,0:T(8,128)(2,1)S(1)}, bf16[256,128]{1,0:T(8,128)(2,1)S(1)}, u32[]{:S(2)}, u32[]{:S(2)}) collective-permute-start(bf16[256,128]{1,0:T(8,128)(2,1)S(1)} %get-tuple-element.33), channel_id=1, source_target_pairs={{0,2},{1,3},{2,0},{3,1},{4,6},{5,7},{6,4},{7,5},{8,10},{9,11},{10,... | collective-permute-start | bytes 196616 | tf_op jit(solution)/shard_map/ppermute | solution.py:492
  20.6 2.6 %collective-permute-start.10 = (bf16[256,128]{1,0:T(8,128)(2,1)S(1)}, bf16[256,128]{1,0:T(8,128)(2,1)S(1)}, u32[]{:S(2)}, u32[]{:S(2)}) collective-permute-start(bf16[256,128]{1,0:T(8,128)(2,1)S(1)} %get-tuple-element.33), channel_id=1, source_target_pairs={{0,4},{1,5},{2,6},{3,7},{4,0},{5,1},{6,2},{7,3},{8,12},{9,13},{10,... | collective-permute-start | bytes 196616 | tf_op jit(solution)/shard_map/ppermute | solution.py:492
  23.1 0.3 collective-permute-start.13
  23.4 0.6 collective-permute-done.18.refs_6_
  24.1 0.9 collective-permute-start.3
  24.9 3.6 %attend_high.1 = (bf16[256,128]{1,0:T(8,128)(2,1)S(1)}, bf16[256,128]{1,0:T(8,128)(2,1)S(1)}, bf16[256,128]{1,0:T(8,128)(2,1)S(1)}, bf16[256,128]{1,0:T(8,128)(2,1)S(1)}) custom-call(s32[2]{0:T(128)S(1)} %pad_add_fusion.ids_ref, bf16[768,128]{1,0:T(8,128)(2,1)S(1)} %get-tuple-element.29.refs_0_, bf16[768,128]{1,0:T(8,128)(2,1)S(1)} %collective-permute-done.refs_1_, ...), custom_call_target="tpu_custom_call" | custom-call | flops 872415232 | bytes 2097152 | tf_op jit(solution)/shard_map/attend_high/pallas_call | solution.py:275
  28.6 1.0 collective-permute-start.24
  29.6 1.8 %collective-permute-start.20 = (bf16[256,128]{1,0:T(8,128)(2,1)S(1)}, bf16[256,128]{1,0:T(8,128)(2,1)S(1)}, u32[]{:S(2)}, u32[]{:S(2)}) collective-permute-start(bf16[256,128]{1,0:T(8,128)(2,1)S(1)} %get-tuple-element.43), channel_id=1, source_target_pairs={{0,8},{8,0},{16,24},{24,16},{1,9},{9,1},{17,25},{25,17},{2,10},{10... | collective-permute-start | bytes 196616 | tf_op jit(solution)/shard_map/ppermute | solution.py:538
  31.4 2.5 %collective-permute-done.20 = bf16[256,128]{1,0:T(8,128)(2,1)S(1)} collective-permute-done((bf16[256,128]{1,0:T(8,128)(2,1)S(1)}, bf16[256,128]{1,0:T(8,128)(2,1)S(1)}, u32[]{:S(2)}, u32[]{:S(2)}) %collective-permute-start.20) | collective-permute-done | bytes 65568 | tf_op jit(solution)/shard_map/ppermute | solution.py:538
  33.9 1.3 %collective-permute-start.4 = (bf16[256,128]{1,0:T(8,128)(2,1)S(1)}, bf16[256,128]{1,0:T(8,128)(2,1)S(1)}, u32[]{:S(2)}, u32[]{:S(2)}) collective-permute-start(bf16[256,128]{1,0:T(8,128)(2,1)S(1)} %get-tuple-element.35), channel_id=1, source_target_pairs={{0,16},{8,24},{16,0},{24,8},{1,17},{9,25},{17,1},{25,9},{2,18},{10... | collective-permute-start | bytes 196616 | tf_op jit(solution)/shard_map/ppermute | solution.py:538
  35.2 3.7 %collective-permute-done.4 = bf16[256,128]{1,0:T(8,128)(2,1)S(1)} collective-permute-done((bf16[256,128]{1,0:T(8,128)(2,1)S(1)}, bf16[256,128]{1,0:T(8,128)(2,1)S(1)}, u32[]{:S(2)}, u32[]{:S(2)}) %collective-permute-start.4) | collective-permute-done | bytes 65568 | tf_op jit(solution)/shard_map/ppermute | solution.py:538
  38.9 2.0 %collective-permute-start.5 = (bf16[256,128]{1,0:T(8,128)(2,1)S(1)}, bf16[256,128]{1,0:T(8,128)(2,1)S(1)}, u32[]{:S(2)}, u32[]{:S(2)}) collective-permute-start(bf16[256,128]{1,0:T(8,128)(2,1)S(1)} %get-tuple-element.36), channel_id=1, source_target_pairs={{0,24},{8,16},{16,8},{24,0},{1,25},{9,17},{17,9},{25,1},{2,26},{10... | collective-permute-start | bytes 196616 | tf_op jit(solution)/shard_map/ppermute | solution.py:538
  41.0 3.1 %collective-permute-done.5 = bf16[256,128]{1,0:T(8,128)(2,1)S(1)} collective-permute-done((bf16[256,128]{1,0:T(8,128)(2,1)S(1)}, bf16[256,128]{1,0:T(8,128)(2,1)S(1)}, u32[]{:S(2)}, u32[]{:S(2)}) %collective-permute-start.5) | collective-permute-done | bytes 65568 | tf_op jit(solution)/shard_map/ppermute | solution.py:538
  44.1 1.0 collective-permute-start.21
  45.1 3.3 %collective-permute-done.21 = bf16[256,128]{1,0:T(8,128)(2,1)S(1)} collective-permute-done((bf16[256,128]{1,0:T(8,128)(2,1)S(1)}, bf16[256,128]{1,0:T(8,128)(2,1)S(1)}, u32[]{:S(2)}, u32[]{:S(2)}) %collective-permute-start.21) | collective-permute-done | bytes 65568 | tf_op jit(solution)/shard_map/ppermute | solution.py:538
  48.3 2.0 %collective-permute-start.22 = (bf16[256,128]{1,0:T(8,128)(2,1)S(1)}, bf16[256,128]{1,0:T(8,128)(2,1)S(1)}, u32[]{:S(2)}, u32[]{:S(2)}) collective-permute-start(bf16[256,128]{1,0:T(8,128)(2,1)S(1)} %get-tuple-element.45), channel_id=1, source_target_pairs={{0,24},{8,16},{16,8},{24,0},{1,25},{9,17},{17,9},{25,1},{2,26},{10... | collective-permute-start | bytes 196616 | tf_op jit(solution)/shard_map/ppermute | solution.py:538
  50.4 3.1 %collective-permute-done.22 = bf16[256,128]{1,0:T(8,128)(2,1)S(1)} collective-permute-done((bf16[256,128]{1,0:T(8,128)(2,1)S(1)}, bf16[256,128]{1,0:T(8,128)(2,1)S(1)}, u32[]{:S(2)}, u32[]{:S(2)}) %collective-permute-start.22) | collective-permute-done | bytes 65568 | tf_op jit(solution)/shard_map/ppermute | solution.py:538
  53.5 3.1 %collective-permute-start.27 = (bf16[256,128]{1,0:T(8,128)(2,1)S(1)}, bf16[256,128]{1,0:T(8,128)(2,1)S(1)}, u32[]{:S(2)}, u32[]{:S(2)}) collective-permute-start(bf16[256,128]{1,0:T(8,128)(2,1)S(1)} %get-tuple-element.42), channel_id=1, source_target_pairs={{0,4},{1,5},{2,6},{3,7},{4,0},{5,1},{6,2},{7,3},{8,12},{9,13},{10,... | collective-permute-start | bytes 196616 | tf_op jit(solution)/shard_map/ppermute | solution.py:492
  56.6 0.3 collective-permute-start.30
  56.9 0.4 collective-permute-start.8
  57.3 3.9 %collective-permute-start.11 = (bf16[768,128]{1,0:T(8,128)(2,1)S(1)}, bf16[768,128]{1,0:T(8,128)(2,1)S(1)}, u32[]{:S(2)}, u32[]{:S(2)}) collective-permute-start(bf16[768,128]{1,0:T(8,128)(2,1)S(1)} %get-tuple-element.59), channel_id=1, source_target_pairs={{0,4},{1,5},{2,6},{3,7},{4,0},{5,1},{6,2},{7,3},{8,12},{9,13},{10,... | collective-permute-start | bytes 589832 | tf_op jit(solution)/shard_map/ppermute | solution.py:492
  61.2 0.7 collective-permute-start.14
  61.9 1.6 %collective-permute-done.30 = bf16[256,128]{1,0:T(8,128)(2,1)S(1)} collective-permute-done((bf16[256,128]{1,0:T(8,128)(2,1)S(1)}, bf16[256,128]{1,0:T(8,128)(2,1)S(1)}, u32[]{:S(2)}, u32[]{:S(2)}) %collective-permute-start.30) | collective-permute-done | bytes 65568 | tf_op jit(solution)/shard_map/ppermute | solution.py:492
  63.5 1.5 %collective-permute-start.25 = (bf16[768,128]{1,0:T(8,128)(2,1)S(1)}, bf16[768,128]{1,0:T(8,128)(2,1)S(1)}, u32[]{:S(2)}, u32[]{:S(2)}) collective-permute-start(bf16[768,128]{1,0:T(8,128)(2,1)S(1)} %get-tuple-element.53), channel_id=1, source_target_pairs={{0,2},{1,3},{2,0},{3,1},{4,6},{5,7},{6,4},{7,5},{8,10},{9,11},{10,... | collective-permute-start | bytes 589832 | tf_op jit(solution)/shard_map/ppermute | solution.py:492
  65.0 5.9 %collective-permute-done.11 = bf16[768,128]{1,0:T(8,128)(2,1)S(1)} collective-permute-done((bf16[768,128]{1,0:T(8,128)(2,1)S(1)}, bf16[768,128]{1,0:T(8,128)(2,1)S(1)}, u32[]{:S(2)}, u32[]{:S(2)}) %collective-permute-start.11) | collective-permute-done | bytes 196640 | tf_op jit(solution)/shard_map/ppermute | solution.py:492
  70.9 1.3 %collective-permute-start.15 = (bf16[768,128]{1,0:T(8,128)(2,1)S(1)}, bf16[768,128]{1,0:T(8,128)(2,1)S(1)}, u32[]{:S(2)}, u32[]{:S(2)}) collective-permute-start(bf16[768,128]{1,0:T(8,128)(2,1)S(1)} %collective-permute-done.11), channel_id=1, source_target_pairs={{2,0},{3,1},{4,6},{5,7},{10,8},{11,9},{12,14},{13,15},{18,16},{19,... | collective-permute-start | bytes 589832 | tf_op jit(solution)/shard_map/ppermute | solution.py:482
  72.3 0.1 collective-permute-start.6
  72.4 2.7 %collective-permute-start.31 = (bf16[768,128]{1,0:T(8,128)(2,1)S(1)}, bf16[768,128]{1,0:T(8,128)(2,1)S(1)}, u32[]{:S(2)}, u32[]{:S(2)}) collective-permute-start(bf16[768,128]{1,0:T(8,128)(2,1)S(1)} %get-tuple-element.53), channel_id=1, source_target_pairs={{0,6},{1,7},{2,4},{3,5},{4,2},{5,3},{6,0},{7,1},{8,14},{9,15},{10,... | collective-permute-start | bytes 589832 | tf_op jit(solution)/shard_map/ppermute | solution.py:492
  75.1 9.3 %collective-permute-done.28 = bf16[768,128]{1,0:T(8,128)(2,1)S(1)} collective-permute-done((bf16[768,128]{1,0:T(8,128)(2,1)S(1)}, bf16[768,128]{1,0:T(8,128)(2,1)S(1)}, u32[]{:S(2)}, u32[]{:S(2)}) %collective-permute-start.28) | collective-permute-done | bytes 196640 | tf_op jit(solution)/shard_map/ppermute | solution.py:492
  84.3 0.4 collective-permute-done.15
  84.8 0.1 collective-permute-start.26
  85.0 0.5 collective-permute-start.9
  85.5 0.2 collective-permute-start.12
  85.6 0.4 collective-permute-start.16
  86.1 0.2 collective-permute-start.29
  86.3 0.4 collective-permute-start.32
  86.7 1.3 %shard_map.139.base_ref = f32[256,512]{1,0:T(8,128)S(1)} custom-call(s32[8]{0:T(128)S(1)} %copy-done.7, s32[2]{0:T(128)S(1)} %pad_add_fusion.ids_ref, bf16[512,512]{1,0:T(8,128)(2,1)S(1)} %copy-done.2, bf16[4096,512]{1,0:T(8,128)(2,1)S(1)} %copy-done, bf16[1024,128]{1,0:T(8,128)(2,1)S(1)} %get-tuple-element.54.refs_0_, ...), custom_call_target="tpu_custom_call" | custom-call | flops 536870912 | bytes 6291456 | tf_op jit(solution)/shard_map/pallas_call | solution.py:332
  88.0 2.0 %shard_map.137 = (f32[256,512]{1,0:T(8,128)S(1)}, bf16[256,512]{1,0:T(8,128)(2,1)S(1)}, f32[1,256]{1,0:T(1,128)S(1)}) custom-call(s32[8]{0:T(128)S(1)} %copy-done.7, s32[2]{0:T(128)S(1)} %pad_add_fusion.ids_ref, bf16[512,512]{1,0:T(8,128)(2,1)S(1)} %copy-done.2, bf16[4096,512]{1,0:T(8,128)(2,1)S(1)} %copy-done, ...), custom_call_target="tpu_custom_call" | custom-call | flops 1073741824 | bytes 6291456 | tf_op jit(solution)/shard_map/pallas_call | solution.py:332
  90.1 1.4 %collective-permute-start.36 = (bf16[256,512]{1,0:T(8,128)(2,1)S(1)}, bf16[256,512]{1,0:T(8,128)(2,1)S(1)}, u32[]{:S(2)}, u32[]{:S(2)}) collective-permute-start(bf16[256,512]{1,0:T(8,128)(2,1)S(1)} %get-tuple-element.51), channel_id=1, source_target_pairs={{0,8},{8,16},{16,24},{24,0},{1,9},{9,17},{17,25},{25,1},{2,10},{10... | collective-permute-start | bytes 786440 | tf_op jit(solution)/shard_map/ppermute | solution.py:557
  91.5 2.0 %shard_map.140 = (f32[256,512]{1,0:T(8,128)S(1)}, bf16[256,512]{1,0:T(8,128)(2,1)}, f32[1,512]{1,0:T(1,128)S(1)}) custom-call(s32[8]{0:T(128)S(1)} %copy-done.7, s32[2]{0:T(128)S(1)} %pad_add_fusion.ids_ref, f32[256,512]{1,0:T(8,128)S(1)} %shard_map.139.base_ref, bf16[4096,512]{1,0:T(8,128)(2,1)S(1)} %copy-done, ...), custom_call_target="tpu_custom_call" | custom-call | flops 536870912 | bytes 6291456 | tf_op jit(solution)/shard_map/pallas_call | solution.py:332
  93.5 1.6 %collective-permute-start.37 = (bf16[256,512]{1,0:T(8,128)(2,1)}, bf16[256,512]{1,0:T(8,128)(2,1)S(1)}, u32[]{:S(2)}, u32[]{:S(2)}) collective-permute-start(bf16[256,512]{1,0:T(8,128)(2,1)} %get-tuple-element.52), channel_id=1, source_target_pairs={{0,24},{8,0},{16,8},{24,16},{1,25},{9,1},{17,9},{25,17},{2,26},{10... | collective-permute-start | bytes 786440 | tf_op jit(solution)/shard_map/ppermute | solution.py:566
  95.1 1.2 %collective-permute-done.33 = f32[1,512]{1,0:T(1,128)S(1)} collective-permute-done((f32[1,512]{1,0:T(1,128)S(1)}, f32[1,512]{1,0:T(1,128)S(1)}, u32[]{:S(2)}, u32[]{:S(2)}) %collective-permute-start.33) | collective-permute-done | bytes 2080 | tf_op jit(solution)/shard_map/ppermute | solution.py:507
  96.2 2.3 %collective-permute-start.34 = (f32[1,512]{1,0:T(1,128)S(1)}, f32[1,512]{1,0:T(1,128)S(1)}, u32[]{:S(2)}, u32[]{:S(2)}) collective-permute-start(f32[1,512]{1,0:T(1,128)S(1)} %add.13), channel_id=1, source_target_pairs={{0,2},{1,3},{2,0},{3,1},{4,6},{5,7},{6,4},{7,5},{8,10},{9,11},{10,... | collective-permute-start | bytes 6152 | tf_op jit(solution)/shard_map/ppermute | solution.py:507
  98.5 0.1 copy.15.len_ref
  98.7 1.4 %collective-permute-done.34 = f32[1,512]{1,0:T(1,128)S(1)} collective-permute-done((f32[1,512]{1,0:T(1,128)S(1)}, f32[1,512]{1,0:T(1,128)S(1)}, u32[]{:S(2)}, u32[]{:S(2)}) %collective-permute-start.34) | collective-permute-done | bytes 2080 | tf_op jit(solution)/shard_map/ppermute | solution.py:507
  100.1 2.2 %collective-permute-start.35 = (f32[1,512]{1,0:T(1,128)S(1)}, f32[1,512]{1,0:T(1,128)S(1)}, u32[]{:S(2)}, u32[]{:S(2)}) collective-permute-start(f32[1,512]{1,0:T(1,128)S(1)} %add.14), channel_id=1, source_target_pairs={{0,4},{1,5},{2,6},{3,7},{4,0},{5,1},{6,2},{7,3},{8,12},{9,13},{10,... | collective-permute-start | bytes 6152 | tf_op jit(solution)/shard_map/ppermute | solution.py:507
  102.3 0.5 spectrum.1.spec_ref
  102.9 1.7 %collective-permute-done.35 = f32[1,512]{1,0:T(1,128)S(1)} collective-permute-done((f32[1,512]{1,0:T(1,128)S(1)}, f32[1,512]{1,0:T(1,128)S(1)}, u32[]{:S(2)}, u32[]{:S(2)}) %collective-permute-start.35) | collective-permute-done | bytes 2080 | tf_op jit(solution)/shard_map/ppermute | solution.py:507
  104.6 0.4 collective-permute-start.38
  105.0 1.3 %collective-permute-start.39 = (f32[1,512]{1,0:T(1,128)S(1)}, f32[1,512]{1,0:T(1,128)S(1)}, u32[]{:S(2)}, u32[]{:S(2)}) collective-permute-start(f32[1,512]{1,0:T(1,128)S(1)} %add.15.sq_ref), channel_id=1, source_target_pairs={{8,16},{16,8},{24,0},{0,24},{9,17},{17,9},{25,1},{1,25},{10,18},{1... | collective-permute-start | bytes 6152 | tf_op jit(solution)/shard_map/ppermute | solution.py:569
  106.3 2.2 %conv_own.1 = (f32[512,512]{1,0:T(8,128)S(1)}, bf16[256,512]{1,0:T(8,128)(2,1)S(1)}) custom-call(f32[256,512]{1,0:T(8,128)S(1)} %get-tuple-element.37.res_low, f32[256,512]{1,0:T(8,128)S(1)} %get-tuple-element.47.res_high, f32[1,512]{1,0:T(1,128)S(1)} %add.15.sq_ref, f32[512,512]{1,0:T(8,128)S(1)} %spectrum.1.spec_ref, f32[1,512]{1,0:T(1,128)S(1)} %bitcast.5, ...), custom_call_target="tpu_custom_call" | custom-call | flops 671088640 | bytes 3145728 | tf_op jit(solution)/shard_map/conv_own/pallas_call | solution.py:571
  108.5 1.0 collective-permute-done.39.sq_b
  109.5 2.7 %conv_last.1 = bf16[512,512]{1,0:T(8,128)(2,1)} custom-call(s32[8]{0:T(128)S(1)} %copy-done.7, s32[2]{0:T(128)S(1)} %pad_add_fusion.ids_ref, f32[512,512]{1,0:T(8,128)S(1)} %get-tuple-element.49.part_ref, bf16[256,512]{1,0:T(8,128)(2,1)S(1)} %get-tuple-element.50.low_ref, bf16[256,512]{1,0:T(8,128)(2,1)S(1)} %collective-permute-done.36.raw_low, ...), custom_call_target="tpu_custom_call" | custom-call | flops 671088640 | bytes 3145728 | tf_op jit(solution)/shard_map/conv_last/pallas_call | solution.py:583
  (73 shorter events, 0.6 us)
Async XLA Ops:
  2.0 10.1 %collective-permute-start = (bf16[768,128]{1,0:T(8,128)(2,1)S(1)}, bf16[768,128]{1,0:T(8,128)(2,1)S(1)}, u32[]{:S(2)}, u32[]{:S(2)}) collective-permute-start(bf16[768,128]{1,0:T(8,128)(2,1)S(1)} %get-tuple-element.30), channel_id=1, source_target_pairs={{0,8},{8,0},{16,24},{24,16},{1,9},{9,1},{17,25},{25,17},{2,10},{10... | collective-permute-start | bytes 589832 | tf_op jit(solution)/shard_map/ppermute | solution.py:538
  5.1 11.0 %collective-permute-start.1 = (bf16[768,128]{1,0:T(8,128)(2,1)S(1)}, bf16[768,128]{1,0:T(8,128)(2,1)S(1)}, u32[]{:S(2)}, u32[]{:S(2)}) collective-permute-start(bf16[768,128]{1,0:T(8,128)(2,1)S(1)} %get-tuple-element.31), channel_id=1, source_target_pairs={{0,16},{8,24},{16,0},{24,8},{1,17},{9,25},{17,1},{25,9},{2,18},{10... | collective-permute-start | bytes 589832 | tf_op jit(solution)/shard_map/ppermute | solution.py:538
  6.6 10.0 %collective-permute-start.2 = (bf16[768,128]{1,0:T(8,128)(2,1)S(1)}, bf16[768,128]{1,0:T(8,128)(2,1)S(1)}, u32[]{:S(2)}, u32[]{:S(2)}) collective-permute-start(bf16[768,128]{1,0:T(8,128)(2,1)S(1)} %get-tuple-element.32), channel_id=1, source_target_pairs={{0,24},{8,16},{16,8},{24,0},{1,25},{9,17},{17,9},{25,1},{2,26},{10... | collective-permute-start | bytes 589832 | tf_op jit(solution)/shard_map/ppermute | solution.py:538
  8.6 14.6 %collective-permute-start.17 = (bf16[768,128]{1,0:T(8,128)(2,1)S(1)}, bf16[768,128]{1,0:T(8,128)(2,1)S(1)}, u32[]{:S(2)}, u32[]{:S(2)}) collective-permute-start(bf16[768,128]{1,0:T(8,128)(2,1)S(1)} %get-tuple-element.39), channel_id=1, source_target_pairs={{0,8},{8,0},{16,24},{24,16},{1,9},{9,1},{17,25},{25,17},{2,10},{10... | collective-permute-start | bytes 589832 | tf_op jit(solution)/shard_map/ppermute | solution.py:538
  10.6 13.5 %collective-permute-start.18 = (bf16[768,128]{1,0:T(8,128)(2,1)S(1)}, bf16[768,128]{1,0:T(8,128)(2,1)S(1)}, u32[]{:S(2)}, u32[]{:S(2)}) collective-permute-start(bf16[768,128]{1,0:T(8,128)(2,1)S(1)} %get-tuple-element.40), channel_id=1, source_target_pairs={{0,16},{8,24},{16,0},{24,8},{1,17},{9,25},{17,1},{25,9},{2,18},{10... | collective-permute-start | bytes 589832 | tf_op jit(solution)/shard_map/ppermute | solution.py:538
  12.1 12.8 %collective-permute-start.19 = (bf16[768,128]{1,0:T(8,128)(2,1)S(1)}, bf16[768,128]{1,0:T(8,128)(2,1)S(1)}, u32[]{:S(2)}, u32[]{:S(2)}) collective-permute-start(bf16[768,128]{1,0:T(8,128)(2,1)S(1)} %get-tuple-element.41), channel_id=1, source_target_pairs={{0,24},{8,16},{16,8},{24,0},{1,25},{9,17},{17,9},{25,1},{2,26},{10... | collective-permute-start | bytes 589832 | tf_op jit(solution)/shard_map/ppermute | solution.py:538
  18.9 67.8 %copy-start = (bf16[4096,512]{1,0:T(8,128)(2,1)S(1)}, bf16[4096,512]{1,0:T(8,128)(2,1)}, u32[]{:S(2)}) copy-start(bf16[4096,512]{1,0:T(8,128)(2,1)} %w_ref.5) | copy-start | bytes 12582916
  18.9 67.8 %copy-start.2 = (bf16[512,512]{1,0:T(8,128)(2,1)S(1)}, bf16[512,512]{1,0:T(8,128)(2,1)}, u32[]{:S(2)}) copy-start(bf16[512,512]{1,0:T(8,128)(2,1)} %base_ref.3) | copy-start | bytes 1572868
  18.9 67.8 %copy-start.7 = (s32[8]{0:T(128)S(1)}, s32[8]{0:T(128)}, u32[]{:S(2)}) copy-start(s32[8]{0:T(128)} %slots_ref.11) | copy-start | bytes 100
  18.9 37.7 %collective-permute-start.7 = (bf16[256,128]{1,0:T(8,128)(2,1)S(1)}, bf16[256,128]{1,0:T(8,128)(2,1)S(1)}, u32[]{:S(2)}, u32[]{:S(2)}) collective-permute-start(bf16[256,128]{1,0:T(8,128)(2,1)S(1)} %get-tuple-element.33), channel_id=1, source_target_pairs={{0,2},{1,3},{2,0},{3,1},{4,6},{5,7},{6,4},{7,5},{8,10},{9,11},{10,... | collective-permute-start | bytes 196616 | tf_op jit(solution)/shard_map/ppermute | solution.py:492
  20.6 36.3 %collective-permute-start.10 = (bf16[256,128]{1,0:T(8,128)(2,1)S(1)}, bf16[256,128]{1,0:T(8,128)(2,1)S(1)}, u32[]{:S(2)}, u32[]{:S(2)}) collective-permute-start(bf16[256,128]{1,0:T(8,128)(2,1)S(1)} %get-tuple-element.33), channel_id=1, source_target_pairs={{0,4},{1,5},{2,6},{3,7},{4,0},{5,1},{6,2},{7,3},{8,12},{9,13},{10,... | collective-permute-start | bytes 196616 | tf_op jit(solution)/shard_map/ppermute | solution.py:492
  23.1 61.8 %collective-permute-start.13 = (bf16[256,128]{1,0:T(8,128)(2,1)S(1)}, bf16[256,128]{1,0:T(8,128)(2,1)S(1)}, u32[]{:S(2)}, u32[]{:S(2)}) collective-permute-start(bf16[256,128]{1,0:T(8,128)(2,1)S(1)} %get-tuple-element.33), channel_id=1, source_target_pairs={{0,6},{1,7},{2,4},{3,5},{4,2},{5,3},{6,0},{7,1},{8,14},{9,15},{10,... | collective-permute-start | bytes 196616 | tf_op jit(solution)/shard_map/ppermute | solution.py:492
  24.1 5.5 %collective-permute-start.3 = (bf16[256,128]{1,0:T(8,128)(2,1)S(1)}, bf16[256,128]{1,0:T(8,128)(2,1)S(1)}, u32[]{:S(2)}, u32[]{:S(2)}) collective-permute-start(bf16[256,128]{1,0:T(8,128)(2,1)S(1)} %get-tuple-element.34), channel_id=1, source_target_pairs={{0,8},{8,0},{16,24},{24,16},{1,9},{9,1},{17,25},{25,17},{2,10},{10... | collective-permute-start | bytes 196616 | tf_op jit(solution)/shard_map/ppermute | solution.py:538
  28.6 28.8 %collective-permute-start.24 = (bf16[256,128]{1,0:T(8,128)(2,1)S(1)}, bf16[256,128]{1,0:T(8,128)(2,1)S(1)}, u32[]{:S(2)}, u32[]{:S(2)}) collective-permute-start(bf16[256,128]{1,0:T(8,128)(2,1)S(1)} %get-tuple-element.42), channel_id=1, source_target_pairs={{0,2},{1,3},{2,0},{3,1},{4,6},{5,7},{6,4},{7,5},{8,10},{9,11},{10,... | collective-permute-start | bytes 196616 | tf_op jit(solution)/shard_map/ppermute | solution.py:492
  29.6 4.3 %collective-permute-start.20 = (bf16[256,128]{1,0:T(8,128)(2,1)S(1)}, bf16[256,128]{1,0:T(8,128)(2,1)S(1)}, u32[]{:S(2)}, u32[]{:S(2)}) collective-permute-start(bf16[256,128]{1,0:T(8,128)(2,1)S(1)} %get-tuple-element.43), channel_id=1, source_target_pairs={{0,8},{8,0},{16,24},{24,16},{1,9},{9,1},{17,25},{25,17},{2,10},{10... | collective-permute-start | bytes 196616 | tf_op jit(solution)/shard_map/ppermute | solution.py:538
  33.9 5.0 %collective-permute-start.4 = (bf16[256,128]{1,0:T(8,128)(2,1)S(1)}, bf16[256,128]{1,0:T(8,128)(2,1)S(1)}, u32[]{:S(2)}, u32[]{:S(2)}) collective-permute-start(bf16[256,128]{1,0:T(8,128)(2,1)S(1)} %get-tuple-element.35), channel_id=1, source_target_pairs={{0,16},{8,24},{16,0},{24,8},{1,17},{9,25},{17,1},{25,9},{2,18},{10... | collective-permute-start | bytes 196616 | tf_op jit(solution)/shard_map/ppermute | solution.py:538
  38.9 5.2 %collective-permute-start.5 = (bf16[256,128]{1,0:T(8,128)(2,1)S(1)}, bf16[256,128]{1,0:T(8,128)(2,1)S(1)}, u32[]{:S(2)}, u32[]{:S(2)}) collective-permute-start(bf16[256,128]{1,0:T(8,128)(2,1)S(1)} %get-tuple-element.36), channel_id=1, source_target_pairs={{0,24},{8,16},{16,8},{24,0},{1,25},{9,17},{17,9},{25,1},{2,26},{10... | collective-permute-start | bytes 196616 | tf_op jit(solution)/shard_map/ppermute | solution.py:538
  44.1 4.3 %collective-permute-start.21 = (bf16[256,128]{1,0:T(8,128)(2,1)S(1)}, bf16[256,128]{1,0:T(8,128)(2,1)S(1)}, u32[]{:S(2)}, u32[]{:S(2)}) collective-permute-start(bf16[256,128]{1,0:T(8,128)(2,1)S(1)} %get-tuple-element.44), channel_id=1, source_target_pairs={{0,16},{8,24},{16,0},{24,8},{1,17},{9,25},{17,1},{25,9},{2,18},{10... | collective-permute-start | bytes 196616 | tf_op jit(solution)/shard_map/ppermute | solution.py:538
  48.3 5.2 %collective-permute-start.22 = (bf16[256,128]{1,0:T(8,128)(2,1)S(1)}, bf16[256,128]{1,0:T(8,128)(2,1)S(1)}, u32[]{:S(2)}, u32[]{:S(2)}) collective-permute-start(bf16[256,128]{1,0:T(8,128)(2,1)S(1)} %get-tuple-element.45), channel_id=1, source_target_pairs={{0,24},{8,16},{16,8},{24,0},{1,25},{9,17},{17,9},{25,1},{2,26},{10... | collective-permute-start | bytes 196616 | tf_op jit(solution)/shard_map/ppermute | solution.py:538
  53.5 7.7 %collective-permute-start.27 = (bf16[256,128]{1,0:T(8,128)(2,1)S(1)}, bf16[256,128]{1,0:T(8,128)(2,1)S(1)}, u32[]{:S(2)}, u32[]{:S(2)}) collective-permute-start(bf16[256,128]{1,0:T(8,128)(2,1)S(1)} %get-tuple-element.42), channel_id=1, source_target_pairs={{0,4},{1,5},{2,6},{3,7},{4,0},{5,1},{6,2},{7,3},{8,12},{9,13},{10,... | collective-permute-start | bytes 196616 | tf_op jit(solution)/shard_map/ppermute | solution.py:492
  56.6 6.9 %collective-permute-start.30 = (bf16[256,128]{1,0:T(8,128)(2,1)S(1)}, bf16[256,128]{1,0:T(8,128)(2,1)S(1)}, u32[]{:S(2)}, u32[]{:S(2)}) collective-permute-start(bf16[256,128]{1,0:T(8,128)(2,1)S(1)} %get-tuple-element.42), channel_id=1, source_target_pairs={{0,6},{1,7},{2,4},{3,5},{4,2},{5,3},{6,0},{7,1},{8,14},{9,15},{10,... | collective-permute-start | bytes 196616 | tf_op jit(solution)/shard_map/ppermute | solution.py:492
  56.9 14.0 %collective-permute-start.8 = (bf16[768,128]{1,0:T(8,128)(2,1)S(1)}, bf16[768,128]{1,0:T(8,128)(2,1)S(1)}, u32[]{:S(2)}, u32[]{:S(2)}) collective-permute-start(bf16[768,128]{1,0:T(8,128)(2,1)S(1)} %get-tuple-element.59), channel_id=1, source_target_pairs={{0,2},{1,3},{2,0},{3,1},{4,6},{5,7},{6,4},{7,5},{8,10},{9,11},{10,... | collective-permute-start | bytes 589832 | tf_op jit(solution)/shard_map/ppermute | solution.py:492
  57.3 13.6 %collective-permute-start.11 = (bf16[768,128]{1,0:T(8,128)(2,1)S(1)}, bf16[768,128]{1,0:T(8,128)(2,1)S(1)}, u32[]{:S(2)}, u32[]{:S(2)}) collective-permute-start(bf16[768,128]{1,0:T(8,128)(2,1)S(1)} %get-tuple-element.59), channel_id=1, source_target_pairs={{0,4},{1,5},{2,6},{3,7},{4,0},{5,1},{6,2},{7,3},{8,12},{9,13},{10,... | collective-permute-start | bytes 589832 | tf_op jit(solution)/shard_map/ppermute | solution.py:492
  61.2 11.2 %collective-permute-start.14 = (bf16[768,128]{1,0:T(8,128)(2,1)S(1)}, bf16[768,128]{1,0:T(8,128)(2,1)S(1)}, u32[]{:S(2)}, u32[]{:S(2)}) collective-permute-start(bf16[768,128]{1,0:T(8,128)(2,1)S(1)} %get-tuple-element.59), channel_id=1, source_target_pairs={{2,4},{3,5},{4,2},{5,3},{10,12},{11,13},{12,10},{13,11},{18,20},{1... | collective-permute-start | bytes 589832 | tf_op jit(solution)/shard_map/ppermute | solution.py:480
  63.5 8.8 %collective-permute-start.25 = (bf16[768,128]{1,0:T(8,128)(2,1)S(1)}, bf16[768,128]{1,0:T(8,128)(2,1)S(1)}, u32[]{:S(2)}, u32[]{:S(2)}) collective-permute-start(bf16[768,128]{1,0:T(8,128)(2,1)S(1)} %get-tuple-element.53), channel_id=1, source_target_pairs={{0,2},{1,3},{2,0},{3,1},{4,6},{5,7},{6,4},{7,5},{8,10},{9,11},{10,... | collective-permute-start | bytes 589832 | tf_op jit(solution)/shard_map/ppermute | solution.py:492
  70.9 13.5 %collective-permute-start.28 = (bf16[768,128]{1,0:T(8,128)(2,1)S(1)}, bf16[768,128]{1,0:T(8,128)(2,1)S(1)}, u32[]{:S(2)}, u32[]{:S(2)}) collective-permute-start(bf16[768,128]{1,0:T(8,128)(2,1)S(1)} %get-tuple-element.53), channel_id=1, source_target_pairs={{0,4},{1,5},{2,6},{3,7},{4,0},{5,1},{6,2},{7,3},{8,12},{9,13},{10,... | collective-permute-start | bytes 589832 | tf_op jit(solution)/shard_map/ppermute | solution.py:492
  70.9 13.8 %collective-permute-start.15 = (bf16[768,128]{1,0:T(8,128)(2,1)S(1)}, bf16[768,128]{1,0:T(8,128)(2,1)S(1)}, u32[]{:S(2)}, u32[]{:S(2)}) collective-permute-start(bf16[768,128]{1,0:T(8,128)(2,1)S(1)} %collective-permute-done.11), channel_id=1, source_target_pairs={{2,0},{3,1},{4,6},{5,7},{10,8},{11,9},{12,14},{13,15},{18,16},{19,... | collective-permute-start | bytes 589832 | tf_op jit(solution)/shard_map/ppermute | solution.py:482
  72.3 13.4 %collective-permute-start.6 = (bf16[1024,128]{1,0:T(8,128)(2,1)S(1)}, bf16[1024,128]{1,0:T(8,128)(2,1)S(1)}, u32[]{:S(2)}, u32[]{:S(2)}) collective-permute-start(bf16[1024,128]{1,0:T(8,128)(2,1)S(1)} %get-tuple-element.60.refs_0_), channel_id=1, source_target_pairs={{0,1},{1,0},{2,3},{3,2},{4,5},{5,4},{6,7},{7,6},{8,9},{9,8},{10,11... | collective-permute-start | bytes 786440 | tf_op jit(solution)/shard_map/ppermute | solution.py:500
  72.4 13.1 %collective-permute-start.31 = (bf16[768,128]{1,0:T(8,128)(2,1)S(1)}, bf16[768,128]{1,0:T(8,128)(2,1)S(1)}, u32[]{:S(2)}, u32[]{:S(2)}) collective-permute-start(bf16[768,128]{1,0:T(8,128)(2,1)S(1)} %get-tuple-element.53), channel_id=1, source_target_pairs={{0,6},{1,7},{2,4},{3,5},{4,2},{5,3},{6,0},{7,1},{8,14},{9,15},{10,... | collective-permute-start | bytes 589832 | tf_op jit(solution)/shard_map/ppermute | solution.py:492
  84.3 1.7 %collective-permute-start.23 = (bf16[1024,128]{1,0:T(8,128)(2,1)S(1)}, bf16[1024,128]{1,0:T(8,128)(2,1)S(1)}, u32[]{:S(2)}, u32[]{:S(2)}) collective-permute-start(bf16[1024,128]{1,0:T(8,128)(2,1)S(1)} %get-tuple-element.54.refs_0_), channel_id=1, source_target_pairs={{0,1},{1,0},{2,3},{3,2},{4,5},{5,4},{6,7},{7,6},{8,9},{9,8},{10,11... | collective-permute-start | bytes 786440 | tf_op jit(solution)/shard_map/ppermute | solution.py:500
  84.8 1.5 %collective-permute-start.26 = (bf16[1024,128]{1,0:T(8,128)(2,1)S(1)}, bf16[1024,128]{1,0:T(8,128)(2,1)S(1)}, u32[]{:S(2)}, u32[]{:S(2)}) collective-permute-start(bf16[1024,128]{1,0:T(8,128)(2,1)S(1)} %constant_dynamic-update-slice_fusion.18.refs_2_), channel_id=1, source_target_pairs={{0,1},{1,0},{2,3},{3,2},{4,5},{5,4},{6,7},{7,6},{8,9},{9,8},{10,11... | collective-permute-start | bytes 786440 | tf_op jit(solution)/shard_map/ppermute | solution.py:500
  85.0 3.0 %collective-permute-start.9 = (bf16[1024,128]{1,0:T(8,128)(2,1)S(1)}, bf16[1024,128]{1,0:T(8,128)(2,1)S(1)}, u32[]{:S(2)}, u32[]{:S(2)}) collective-permute-start(bf16[1024,128]{1,0:T(8,128)(2,1)S(1)} %constant_dynamic-update-slice_fusion.7.refs_2_), channel_id=1, source_target_pairs={{0,1},{1,0},{2,3},{3,2},{4,5},{5,4},{6,7},{7,6},{8,9},{9,8},{10,11... | collective-permute-start | bytes 786440 | tf_op jit(solution)/shard_map/ppermute | solution.py:500
  85.5 2.5 %collective-permute-start.12 = (bf16[1024,128]{1,0:T(8,128)(2,1)S(1)}, bf16[1024,128]{1,0:T(8,128)(2,1)S(1)}, u32[]{:S(2)}, u32[]{:S(2)}) collective-permute-start(bf16[1024,128]{1,0:T(8,128)(2,1)S(1)} %constant_dynamic-update-slice_fusion.9.refs_4_), channel_id=1, source_target_pairs={{0,1},{1,0},{2,3},{3,2},{4,5},{5,4},{6,7},{7,6},{8,9},{9,8},{10,11... | collective-permute-start | bytes 786440 | tf_op jit(solution)/shard_map/ppermute | solution.py:500
  85.6 2.4 %collective-permute-start.16 = (bf16[1024,128]{1,0:T(8,128)(2,1)S(1)}, bf16[1024,128]{1,0:T(8,128)(2,1)S(1)}, u32[]{:S(2)}, u32[]{:S(2)}) collective-permute-start(bf16[1024,128]{1,0:T(8,128)(2,1)S(1)} %pad_maximum_fusion.refs_6_), channel_id=1, source_target_pairs={{0,1},{1,0},{2,3},{3,2},{4,5},{5,4},{6,7},{7,6},{8,9},{9,8},{10,11... | collective-permute-start | bytes 786440 | tf_op jit(solution)/shard_map/ppermute | solution.py:500
  86.1 5.4 %collective-permute-start.29 = (bf16[1024,128]{1,0:T(8,128)(2,1)S(1)}, bf16[1024,128]{1,0:T(8,128)(2,1)S(1)}, u32[]{:S(2)}, u32[]{:S(2)}) collective-permute-start(bf16[1024,128]{1,0:T(8,128)(2,1)S(1)} %constant_dynamic-update-slice_fusion.20.refs_0_), channel_id=1, source_target_pairs={{0,1},{1,0},{2,3},{3,2},{4,5},{5,4},{6,7},{7,6},{8,9},{9,8},{10,11... | collective-permute-start | bytes 786440 | tf_op jit(solution)/shard_map/ppermute | solution.py:500
  86.3 5.2 %collective-permute-start.32 = (bf16[1024,128]{1,0:T(8,128)(2,1)S(1)}, bf16[1024,128]{1,0:T(8,128)(2,1)S(1)}, u32[]{:S(2)}, u32[]{:S(2)}) collective-permute-start(bf16[1024,128]{1,0:T(8,128)(2,1)S(1)} %constant_dynamic-update-slice_fusion.22.refs_2_), channel_id=1, source_target_pairs={{0,1},{1,0},{2,3},{3,2},{4,5},{5,4},{6,7},{7,6},{8,9},{9,8},{10,11... | collective-permute-start | bytes 786440 | tf_op jit(solution)/shard_map/ppermute | solution.py:500
  90.0 8.5 %copy-start.10 = (s32[512]{0:T(512)S(1)}, s32[512]{0:T(512)}, u32[]{:S(2)}) copy-start(s32[512]{0:T(512)} %param.21) | copy-start | bytes 6148
  90.0 12.3 %copy-start.1 = (bf16[512,256]{1,0:T(8,128)(2,1)S(1)}, bf16[512,256]{1,0:T(8,128)(2,1)}, u32[]{:S(2)}) copy-start(bf16[512,256]{1,0:T(8,128)(2,1)} %constant.16.clone.fh_ref.fh) | copy-start | bytes 786436
  90.0 12.3 %copy-start.4 = (bf16[512,256]{1,0:T(8,128)(2,1)S(1)}, bf16[512,256]{1,0:T(8,128)(2,1)}, u32[]{:S(2)}) copy-start(bf16[512,256]{1,0:T(8,128)(2,1)} %constant.17.clone.fl_ref.fl) | copy-start | bytes 786436
  90.0 12.3 %copy-start.5 = (bf16[512,256]{1,0:T(8,128)(2,1)S(1)}, bf16[512,256]{1,0:T(8,128)(2,1)}, u32[]{:S(2)}) copy-start(bf16[512,256]{1,0:T(8,128)(2,1)} %filters_ref.1) | copy-start | bytes 786436
  90.0 16.3 %copy-start.3 = (bf16[256,512]{1,0:T(8,128)(2,1)S(1)}, bf16[256,512]{1,0:T(8,128)(2,1)}, u32[]{:S(2)}) copy-start(bf16[256,512]{1,0:T(8,128)(2,1)} %constant.18.clone.gh) | copy-start | bytes 786436
  90.0 16.3 %copy-start.6 = (bf16[256,512]{1,0:T(8,128)(2,1)S(1)}, bf16[256,512]{1,0:T(8,128)(2,1)}, u32[]{:S(2)}) copy-start(bf16[256,512]{1,0:T(8,128)(2,1)} %constant.19.clone.gl) | copy-start | bytes 786436
  90.1 16.3 %copy-start.8 = (f32[512]{0:T(512)S(1)}, f32[512]{0:T(512)}, u32[]{:S(2)}) copy-start(f32[512]{0:T(512)} %param.19) | copy-start | bytes 6148
  90.1 16.3 %copy-start.9 = (f32[512]{0:T(512)S(1)}, f32[512]{0:T(512)}, u32[]{:S(2)}) copy-start(f32[512]{0:T(512)} %param.22) | copy-start | bytes 6148
  90.1 19.4 %collective-permute-start.36 = (bf16[256,512]{1,0:T(8,128)(2,1)S(1)}, bf16[256,512]{1,0:T(8,128)(2,1)S(1)}, u32[]{:S(2)}, u32[]{:S(2)}) collective-permute-start(bf16[256,512]{1,0:T(8,128)(2,1)S(1)} %get-tuple-element.51), channel_id=1, source_target_pairs={{0,8},{8,16},{16,24},{24,0},{1,9},{9,17},{17,25},{25,1},{2,10},{10... | collective-permute-start | bytes 786440 | tf_op jit(solution)/shard_map/ppermute | solution.py:557
  93.5 16.0 %collective-permute-start.37 = (bf16[256,512]{1,0:T(8,128)(2,1)}, bf16[256,512]{1,0:T(8,128)(2,1)S(1)}, u32[]{:S(2)}, u32[]{:S(2)}) collective-permute-start(bf16[256,512]{1,0:T(8,128)(2,1)} %get-tuple-element.52), channel_id=1, source_target_pairs={{0,24},{8,0},{16,8},{24,16},{1,25},{9,1},{17,9},{25,17},{2,26},{10... | collective-permute-start | bytes 786440 | tf_op jit(solution)/shard_map/ppermute | solution.py:566
  95.1 1.2 %collective-permute-start.33 = (f32[1,512]{1,0:T(1,128)S(1)}, f32[1,512]{1,0:T(1,128)S(1)}, u32[]{:S(2)}, u32[]{:S(2)}) collective-permute-start(f32[1,512]{1,0:T(1,128)S(1)} %get-tuple-element.48), channel_id=1, source_target_pairs={{0,1},{1,0},{2,3},{3,2},{4,5},{5,4},{6,7},{7,6},{8,9},{9,8},{10,11... | collective-permute-start | bytes 6152 | tf_op jit(solution)/shard_map/ppermute | solution.py:507
  96.2 3.8 %collective-permute-start.34 = (f32[1,512]{1,0:T(1,128)S(1)}, f32[1,512]{1,0:T(1,128)S(1)}, u32[]{:S(2)}, u32[]{:S(2)}) collective-permute-start(f32[1,512]{1,0:T(1,128)S(1)} %add.13), channel_id=1, source_target_pairs={{0,2},{1,3},{2,0},{3,1},{4,6},{5,7},{6,4},{7,5},{8,10},{9,11},{10,... | collective-permute-start | bytes 6152 | tf_op jit(solution)/shard_map/ppermute | solution.py:507
  100.1 4.5 %collective-permute-start.35 = (f32[1,512]{1,0:T(1,128)S(1)}, f32[1,512]{1,0:T(1,128)S(1)}, u32[]{:S(2)}, u32[]{:S(2)}) collective-permute-start(f32[1,512]{1,0:T(1,128)S(1)} %add.14), channel_id=1, source_target_pairs={{0,4},{1,5},{2,6},{3,7},{4,0},{5,1},{6,2},{7,3},{8,12},{9,13},{10,... | collective-permute-start | bytes 6152 | tf_op jit(solution)/shard_map/ppermute | solution.py:507
  104.6 3.9 %collective-permute-start.38 = (f32[1,512]{1,0:T(1,128)S(1)}, f32[1,512]{1,0:T(1,128)S(1)}, u32[]{:S(2)}, u32[]{:S(2)}) collective-permute-start(f32[1,512]{1,0:T(1,128)S(1)} %add.15.sq_ref), channel_id=1, source_target_pairs={{0,8},{8,0},{16,24},{24,16},{1,9},{9,1},{17,25},{25,17},{2,10},{10... | collective-permute-start | bytes 6152 | tf_op jit(solution)/shard_map/ppermute | solution.py:568
  105.0 4.5 %collective-permute-start.39 = (f32[1,512]{1,0:T(1,128)S(1)}, f32[1,512]{1,0:T(1,128)S(1)}, u32[]{:S(2)}, u32[]{:S(2)}) collective-permute-start(f32[1,512]{1,0:T(1,128)S(1)} %add.15.sq_ref), channel_id=1, source_target_pairs={{8,16},{16,8},{24,0},{0,24},{9,17},{17,9},{25,1},{1,25},{10,18},{1... | collective-permute-start | bytes 6152 | tf_op jit(solution)/shard_map/ppermute | solution.py:569

commit v2 on v1

--- a/solution.py
+++ b/solution.py
@@ -547,8 +547,11 @@
     late = gather_mp(jnp.concatenate(att_low[1:], axis=0), mp_size, True)
     parts_low = with_sibling([jnp.concatenate(p, axis=0) for p in zip(early, late)], mp_size)
     att_high = exchange(attend(n, 1, rows, ids, low + high))
-    early = gather_mp(att_high[0], mp_size, False)
-    late = gather_mp(jnp.concatenate(att_high[1:], axis=0), mp_size, False)
+    middle = n // 2
+    own_a = jnp.concatenate(att_high[:middle], axis=0)
+    own_b = jnp.concatenate(att_high[middle:], axis=0)
+    early = gather_mp(own_a, mp_size, True)
+    late = gather_mp(own_b, mp_size, False)
     parts_high = with_sibling([jnp.concatenate(p, axis=0) for p in zip(early, late)], mp_size)
 
     most = mp_size // 2

time: 112 us -> 107 us (0.955)
  waiting for transfers between devices: 41.5 us -> 34.2 us
  starting transfers between devices: 49.1 us -> 51.1 us
    ppermute x12, waiting for transfers between devices: 19.1 us -> 5.21 us  [exchange(): lax.ppermute(pieces[k], 'seq', xor_route(n, k))]
    ppermute x1 -> x2, waiting for transfers between devices: 0.42 us -> 6.51 us  [relayed_piece(): return direct + lax.ppermute(near, 'mp', ends)]
    ppermute x12, starting transfers between devices: 18.8 us -> 17 us  [exchange(): lax.ppermute(pieces[k], 'seq', xor_route(n, k))]
    ppermute x1, starting transfers between devices: 1.4 us -> 3.15 us  [fast_device(): raw_low = lax.ppermute(raw_low, 'seq', ring(n, 1))]
    ppermute x1, starting transfers between devices: 0.45 us -> 2.02 us  [fast_device(): sq_a = lax.ppermute(squares, 'seq', pairs(n, 0))]
    ppermute x1, starting transfers between devices: 1.57 us -> 0.01 us  [fast_device(): raw_high = lax.ppermute(raw_high, 'seq', ring(n, -1))]
    ppermute x1 -> x2, starting transfers between devices: 1.29 us -> 2.57 us  [relayed_piece(): return direct + lax.ppermute(near, 'mp', ends)]
    ppermute x11 -> x10, waiting for transfers between devices: 16.7 us -> 17 us  [gather_mp(): pieces.append(lax.ppermute(own, 'mp', xor_route(size, 2 * k)))]
  transfers between devices with their start and end apart: 40 -> 41, of which waited for: 16 -> 12; matrix products, arithmetic and copies ran while one was open for 0% -> 1% of each run, Pallas kernels for 14% -> 15%
where the time goes in v2:
time: 107 us
  starting transfers between devices  51.1 us (48%)
  waiting for transfers between devices  34.2 us (32%)
  Pallas kernels  20.4 us (19%)
    ppermute x10, starting transfers between devices, gather_mp(): pieces.append(lax.ppermute(own, 'mp', xor_route(size, 2 * k)))  17.2 us
    ppermute x10, waiting for transfers between devices, gather_mp(): pieces.append(lax.ppermute(own, 'mp', xor_route(size, 2 * k)))  17 us
    ppermute x12, starting transfers between devices, exchange(): lax.ppermute(pieces[k], 'seq', xor_route(n, k))  17 us
    ppermute x2, waiting for transfers between devices, relayed_piece(): return direct + lax.ppermute(near, 'mp', ends)  6.51 us
    pallas_call x2, Pallas kernels, attend(): pl.pallas_call(functools.partial(attend_kernel, n, high, rows), out_shape...  5.9 us
    pallas_call x3, Pallas kernels, project(): pl.pallas_call(functools.partial(project_kernel, n, high, indices, len(ex...  5.27 us
    ppermute x12, waiting for transfers between devices, exchange(): lax.ppermute(pieces[k], 'seq', xor_route(n, k))  5.21 us
    ppermute x3, starting transfers between devices, total_mp(): part = part + lax.ppermute(part, 'mp', xor_route(size, k))  5.15 us
  transfers between devices with their start and end apart: 41, of which 12 were waited for; matrix products, arithmetic and copies ran while one was open for 1% of the time, Pallas kernels for 15%

profile of v2, /device:TPU:0, one launch (start us, length us, event | category | flops | bytes accessed | tf_op | source)
XLA Modules:
  0.0 106.8 jit_solution(9965340704094372228)
XLA Ops:
  0.0 0.1 pad_add_fusion.ids_ref
  0.1 2.0 %shard_map.136 = (bf16[768,128]{1,0:T(8,128)(2,1)S(1)}, bf16[768,128]{1,0:T(8,128)(2,1)S(1)}, bf16[768,128]{1,0:T(8,128)(2,1)S(1)}, bf16[768,128]{1,0:T(8,128)(2,1)S(1)}) custom-call(s32[8]{0:T(128)} %slots_ref.11, s32[2]{0:T(128)S(1)} %pad_add_fusion.ids_ref, bf16[512,512]{1,0:T(8,128)(2,1)} %q_ref.3, bf16[512,512]{1,0:T(8,128)(2,1)} %k_ref.3, ...), custom_call_target="tpu_custom_call" | custom-call | bytes 1572864 | tf_op jit(solution)/shard_map/pallas_call | solution.py:203
  2.0 3.0 %collective-permute-start = (bf16[768,128]{1,0:T(8,128)(2,1)S(1)}, bf16[768,128]{1,0:T(8,128)(2,1)S(1)}, u32[]{:S(2)}, u32[]{:S(2)}) collective-permute-start(bf16[768,128]{1,0:T(8,128)(2,1)S(1)} %get-tuple-element.30), channel_id=1, source_target_pairs={{0,8},{8,0},{16,24},{24,16},{1,9},{9,1},{17,25},{25,17},{2,10},{10... | collective-permute-start | bytes 589832 | tf_op jit(solution)/shard_map/ppermute | solution.py:538
  5.1 1.5 %collective-permute-start.1 = (bf16[768,128]{1,0:T(8,128)(2,1)S(1)}, bf16[768,128]{1,0:T(8,128)(2,1)S(1)}, u32[]{:S(2)}, u32[]{:S(2)}) collective-permute-start(bf16[768,128]{1,0:T(8,128)(2,1)S(1)} %get-tuple-element.31), channel_id=1, source_target_pairs={{0,16},{8,24},{16,0},{24,8},{1,17},{9,25},{17,1},{25,9},{2,18},{10... | collective-permute-start | bytes 589832 | tf_op jit(solution)/shard_map/ppermute | solution.py:538
  6.6 0.0 collective-permute-start.2
  6.6 2.0 %shard_map.138 = (bf16[768,128]{1,0:T(8,128)(2,1)S(1)}, bf16[768,128]{1,0:T(8,128)(2,1)S(1)}, bf16[768,128]{1,0:T(8,128)(2,1)S(1)}, bf16[768,128]{1,0:T(8,128)(2,1)S(1)}) custom-call(s32[8]{0:T(128)} %slots_ref.11, s32[2]{0:T(128)S(1)} %pad_add_fusion.ids_ref, bf16[512,512]{1,0:T(8,128)(2,1)} %q_ref.3, bf16[512,512]{1,0:T(8,128)(2,1)} %k_ref.3, ...), custom_call_target="tpu_custom_call" | custom-call | bytes 1572864 | tf_op jit(solution)/shard_map/pallas_call | solution.py:203
  8.6 2.0 %collective-permute-start.17 = (bf16[768,128]{1,0:T(8,128)(2,1)S(1)}, bf16[768,128]{1,0:T(8,128)(2,1)S(1)}, u32[]{:S(2)}, u32[]{:S(2)}) collective-permute-start(bf16[768,128]{1,0:T(8,128)(2,1)S(1)} %get-tuple-element.39), channel_id=1, source_target_pairs={{0,8},{8,0},{16,24},{24,16},{1,9},{9,1},{17,25},{25,17},{2,10},{10... | collective-permute-start | bytes 589832 | tf_op jit(solution)/shard_map/ppermute | solution.py:538
  10.6 1.5 %collective-permute-start.18 = (bf16[768,128]{1,0:T(8,128)(2,1)S(1)}, bf16[768,128]{1,0:T(8,128)(2,1)S(1)}, u32[]{:S(2)}, u32[]{:S(2)}) collective-permute-start(bf16[768,128]{1,0:T(8,128)(2,1)S(1)} %get-tuple-element.40), channel_id=1, source_target_pairs={{0,16},{8,24},{16,0},{24,8},{1,17},{9,25},{17,1},{25,9},{2,18},{10... | collective-permute-start | bytes 589832 | tf_op jit(solution)/shard_map/ppermute | solution.py:538
  12.1 1.7 %collective-permute-start.19 = (bf16[768,128]{1,0:T(8,128)(2,1)S(1)}, bf16[768,128]{1,0:T(8,128)(2,1)S(1)}, u32[]{:S(2)}, u32[]{:S(2)}) collective-permute-start(bf16[768,128]{1,0:T(8,128)(2,1)S(1)} %get-tuple-element.41), channel_id=1, source_target_pairs={{0,24},{8,16},{16,8},{24,0},{1,25},{9,17},{17,9},{25,1},{2,26},{10... | collective-permute-start | bytes 589832 | tf_op jit(solution)/shard_map/ppermute | solution.py:538
  13.8 2.3 %collective-permute-done.1.refs_2_ = bf16[768,128]{1,0:T(8,128)(2,1)S(1)} collective-permute-done((bf16[768,128]{1,0:T(8,128)(2,1)S(1)}, bf16[768,128]{1,0:T(8,128)(2,1)S(1)}, u32[]{:S(2)}, u32[]{:S(2)}) %collective-permute-start.1) | collective-permute-done | bytes 196640 | tf_op jit(solution)/shard_map/ppermute | solution.py:538
  16.1 0.5 collective-permute-done.2.refs_3_
  16.6 2.3 %attend_low.1 = (bf16[256,128]{1,0:T(8,128)(2,1)S(1)}, bf16[256,128]{1,0:T(8,128)(2,1)S(1)}, bf16[256,128]{1,0:T(8,128)(2,1)S(1)}, bf16[256,128]{1,0:T(8,128)(2,1)S(1)}) custom-call(s32[2]{0:T(128)S(1)} %pad_add_fusion.ids_ref, bf16[768,128]{1,0:T(8,128)(2,1)S(1)} %get-tuple-element.29.refs_0_, bf16[768,128]{1,0:T(8,128)(2,1)S(1)} %collective-permute-done.refs_1_, ...), custom_call_target="tpu_custom_call" | custom-call | flops 335544320 | bytes 1048576 | tf_op jit(solution)/shard_map/attend_low/pallas_call | solution.py:275
  18.9 1.6 %collective-permute-start.7 = (bf16[256,128]{1,0:T(8,128)(2,1)S(1)}, bf16[256,128]{1,0:T(8,128)(2,1)S(1)}, u32[]{:S(2)}, u32[]{:S(2)}) collective-permute-start(bf16[256,128]{1,0:T(8,128)(2,1)S(1)} %get-tuple-element.33), channel_id=1, source_target_pairs={{0,2},{1,3},{2,0},{3,1},{4,6},{5,7},{6,4},{7,5},{8,10},{9,11},{10,... | collective-permute-start | bytes 196616 | tf_op jit(solution)/shard_map/ppermute | solution.py:492
  20.5 2.6 %collective-permute-start.10 = (bf16[256,128]{1,0:T(8,128)(2,1)S(1)}, bf16[256,128]{1,0:T(8,128)(2,1)S(1)}, u32[]{:S(2)}, u32[]{:S(2)}) collective-permute-start(bf16[256,128]{1,0:T(8,128)(2,1)S(1)} %get-tuple-element.33), channel_id=1, source_target_pairs={{0,4},{1,5},{2,6},{3,7},{4,0},{5,1},{6,2},{7,3},{8,12},{9,13},{10,... | collective-permute-start | bytes 196616 | tf_op jit(solution)/shard_map/ppermute | solution.py:492
  23.1 1.5 %collective-permute-start.3 = (bf16[256,128]{1,0:T(8,128)(2,1)S(1)}, bf16[256,128]{1,0:T(8,128)(2,1)S(1)}, u32[]{:S(2)}, u32[]{:S(2)}) collective-permute-start(bf16[256,128]{1,0:T(8,128)(2,1)S(1)} %get-tuple-element.34), channel_id=1, source_target_pairs={{0,8},{8,0},{16,24},{24,16},{1,9},{9,1},{17,25},{25,17},{2,10},{10... | collective-permute-start | bytes 196616 | tf_op jit(solution)/shard_map/ppermute | solution.py:538
  24.6 1.7 %collective-permute-start.4 = (bf16[256,128]{1,0:T(8,128)(2,1)S(1)}, bf16[256,128]{1,0:T(8,128)(2,1)S(1)}, u32[]{:S(2)}, u32[]{:S(2)}) collective-permute-start(bf16[256,128]{1,0:T(8,128)(2,1)S(1)} %get-tuple-element.35), channel_id=1, source_target_pairs={{0,16},{8,24},{16,0},{24,8},{1,17},{9,25},{17,1},{25,9},{2,18},{10... | collective-permute-start | bytes 196616 | tf_op jit(solution)/shard_map/ppermute | solution.py:538
  26.3 0.3 collective-permute-start.5
  26.6 3.6 %attend_high.1 = (bf16[256,128]{1,0:T(8,128)(2,1)S(1)}, bf16[256,128]{1,0:T(8,128)(2,1)S(1)}, bf16[256,128]{1,0:T(8,128)(2,1)S(1)}, bf16[256,128]{1,0:T(8,128)(2,1)S(1)}) custom-call(s32[2]{0:T(128)S(1)} %pad_add_fusion.ids_ref, bf16[768,128]{1,0:T(8,128)(2,1)S(1)} %get-tuple-element.29.refs_0_, bf16[768,128]{1,0:T(8,128)(2,1)S(1)} %collective-permute-done.refs_1_, ...), custom_call_target="tpu_custom_call" | custom-call | flops 872415232 | bytes 2097152 | tf_op jit(solution)/shard_map/attend_high/pallas_call | solution.py:275
  30.3 1.8 %collective-permute-start.21 = (bf16[256,128]{1,0:T(8,128)(2,1)S(1)}, bf16[256,128]{1,0:T(8,128)(2,1)S(1)}, u32[]{:S(2)}, u32[]{:S(2)}) collective-permute-start(bf16[256,128]{1,0:T(8,128)(2,1)S(1)} %get-tuple-element.44), channel_id=1, source_target_pairs={{0,16},{8,24},{16,0},{24,8},{1,17},{9,25},{17,1},{25,9},{2,18},{10... | collective-permute-start | bytes 196616 | tf_op jit(solution)/shard_map/ppermute | solution.py:538
  32.1 1.5 %collective-permute-start.20 = (bf16[256,128]{1,0:T(8,128)(2,1)S(1)}, bf16[256,128]{1,0:T(8,128)(2,1)S(1)}, u32[]{:S(2)}, u32[]{:S(2)}) collective-permute-start(bf16[256,128]{1,0:T(8,128)(2,1)S(1)} %get-tuple-element.43), channel_id=1, source_target_pairs={{0,8},{8,0},{16,24},{24,16},{1,9},{9,1},{17,25},{25,17},{2,10},{10... | collective-permute-start | bytes 196616 | tf_op jit(solution)/shard_map/ppermute | solution.py:538
  33.7 0.4 collective-permute-start.22
  34.0 2.4 %collective-permute-done.20 = bf16[256,128]{1,0:T(8,128)(2,1)S(1)} collective-permute-done((bf16[256,128]{1,0:T(8,128)(2,1)S(1)}, bf16[256,128]{1,0:T(8,128)(2,1)S(1)}, u32[]{:S(2)}, u32[]{:S(2)}) %collective-permute-start.20) | collective-permute-done | bytes 65568 | tf_op jit(solution)/shard_map/ppermute | solution.py:538
  36.5 1.0 collective-permute-start.8
  37.5 2.6 %collective-permute-start.11 = (bf16[768,128]{1,0:T(8,128)(2,1)S(1)}, bf16[768,128]{1,0:T(8,128)(2,1)S(1)}, u32[]{:S(2)}, u32[]{:S(2)}) collective-permute-start(bf16[768,128]{1,0:T(8,128)(2,1)S(1)} %get-tuple-element.61), channel_id=1, source_target_pairs={{0,4},{1,5},{2,6},{3,7},{4,0},{5,1},{6,2},{7,3},{8,12},{9,13},{10,... | collective-permute-start | bytes 589832 | tf_op jit(solution)/shard_map/ppermute | solution.py:492
  40.2 0.7 collective-permute-start.14
  40.9 3.2 %collective-permute-start.24 = (bf16[512,128]{1,0:T(8,128)(2,1)S(1)}, bf16[512,128]{1,0:T(8,128)(2,1)S(1)}, u32[]{:S(2)}, u32[]{:S(2)}) collective-permute-start(bf16[512,128]{1,0:T(8,128)(2,1)S(1)} %get-tuple-element.57), channel_id=1, source_target_pairs={{0,2},{1,3},{2,0},{3,1},{4,6},{5,7},{6,4},{7,5},{8,10},{9,11},{10,... | collective-permute-start | bytes 393224 | tf_op jit(solution)/shard_map/ppermute | solution.py:492
  44.0 0.1 collective-permute-start.27
  44.2 4.6 %collective-permute-done.24 = bf16[512,128]{1,0:T(8,128)(2,1)S(1)} collective-permute-done((bf16[512,128]{1,0:T(8,128)(2,1)S(1)}, bf16[512,128]{1,0:T(8,128)(2,1)S(1)}, u32[]{:S(2)}, u32[]{:S(2)}) %collective-permute-start.24) | collective-permute-done | bytes 131104 | tf_op jit(solution)/shard_map/ppermute | solution.py:492
  48.8 2.1 %collective-permute-start.25 = (bf16[512,128]{1,0:T(8,128)(2,1)S(1)}, bf16[512,128]{1,0:T(8,128)(2,1)S(1)}, u32[]{:S(2)}, u32[]{:S(2)}) collective-permute-start(bf16[512,128]{1,0:T(8,128)(2,1)S(1)} %get-tuple-element.53), channel_id=1, source_target_pairs={{0,2},{1,3},{2,0},{3,1},{4,6},{5,7},{6,4},{7,5},{8,10},{9,11},{10,... | collective-permute-start | bytes 393224 | tf_op jit(solution)/shard_map/ppermute | solution.py:492
  50.9 5.8 %collective-permute-done.27 = bf16[512,128]{1,0:T(8,128)(2,1)S(1)} collective-permute-done((bf16[512,128]{1,0:T(8,128)(2,1)S(1)}, bf16[512,128]{1,0:T(8,128)(2,1)S(1)}, u32[]{:S(2)}, u32[]{:S(2)}) %collective-permute-start.27) | collective-permute-done | bytes 131104 | tf_op jit(solution)/shard_map/ppermute | solution.py:492
  56.7 0.7 collective-permute-start.30
  57.4 6.6 %collective-permute-done.28 = bf16[512,128]{1,0:T(8,128)(2,1)S(1)} collective-permute-done((bf16[512,128]{1,0:T(8,128)(2,1)S(1)}, bf16[512,128]{1,0:T(8,128)(2,1)S(1)}, u32[]{:S(2)}, u32[]{:S(2)}) %collective-permute-start.28) | collective-permute-done | bytes 131104 | tf_op jit(solution)/shard_map/ppermute | solution.py:492
  64.0 1.3 %collective-permute-start.31 = (bf16[512,128]{1,0:T(8,128)(2,1)S(1)}, bf16[512,128]{1,0:T(8,128)(2,1)S(1)}, u32[]{:S(2)}, u32[]{:S(2)}) collective-permute-start(bf16[512,128]{1,0:T(8,128)(2,1)S(1)} %collective-permute-done.27), channel_id=1, source_target_pairs={{2,0},{3,1},{4,6},{5,7},{10,8},{11,9},{12,14},{13,15},{18,16},{19,... | collective-permute-start | bytes 393224 | tf_op jit(solution)/shard_map/ppermute | solution.py:482
  65.3 1.3 %collective-permute-start.15 = (bf16[768,128]{1,0:T(8,128)(2,1)S(1)}, bf16[768,128]{1,0:T(8,128)(2,1)S(1)}, u32[]{:S(2)}, u32[]{:S(2)}) collective-permute-start(bf16[768,128]{1,0:T(8,128)(2,1)S(1)} %collective-permute-done.11), channel_id=1, source_target_pairs={{2,0},{3,1},{4,6},{5,7},{10,8},{11,9},{12,14},{13,15},{18,16},{19,... | collective-permute-start | bytes 589832 | tf_op jit(solution)/shard_map/ppermute | solution.py:482
  66.7 0.1 collective-permute-start.6
  66.8 2.1 %collective-permute-start.13 = (bf16[256,128]{1,0:T(8,128)(2,1)S(1)}, bf16[256,128]{1,0:T(8,128)(2,1)S(1)}, u32[]{:S(2)}, u32[]{:S(2)}) collective-permute-start(bf16[256,128]{1,0:T(8,128)(2,1)S(1)} %get-tuple-element.33), channel_id=1, source_target_pairs={{0,6},{1,7},{2,4},{3,5},{4,2},{5,3},{6,0},{7,1},{8,14},{9,15},{10,... | collective-permute-start | bytes 196616 | tf_op jit(solution)/shard_map/ppermute | solution.py:492
  68.9 1.8 %collective-permute-start.32 = (bf16[512,128]{1,0:T(8,128)(2,1)S(1)}, bf16[512,128]{1,0:T(8,128)(2,1)S(1)}, u32[]{:S(2)}, u32[]{:S(2)}) collective-permute-start(bf16[512,128]{1,0:T(8,128)(2,1)S(1)} %get-tuple-element.53), channel_id=1, source_target_pairs={{0,6},{1,7},{2,4},{3,5},{4,2},{5,3},{6,0},{7,1},{8,14},{9,15},{10,... | collective-permute-start | bytes 393224 | tf_op jit(solution)/shard_map/ppermute | solution.py:492
  70.7 0.2 collective-permute-done.31
  70.9 6.3 %collective-permute-done.15 = bf16[768,128]{1,0:T(8,128)(2,1)S(1)} collective-permute-done((bf16[768,128]{1,0:T(8,128)(2,1)S(1)}, bf16[768,128]{1,0:T(8,128)(2,1)S(1)}, u32[]{:S(2)}, u32[]{:S(2)}) %collective-permute-start.15) | collective-permute-done | bytes 196640 | tf_op jit(solution)/shard_map/ppermute | solution.py:482
  77.3 0.1 add.15
  77.4 0.6 collective-permute-start.9
  78.0 0.1 collective-permute-start.12
  78.0 0.5 collective-permute-start.16
  78.6 0.2 collective-permute-start.29
  78.7 0.0 collective-permute-done.26.refs_3_
  78.7 0.4 collective-permute-start.33
  79.2 1.3 %shard_map.139.base_ref = f32[256,512]{1,0:T(8,128)S(1)} custom-call(s32[8]{0:T(128)S(1)} %copy-done.7, s32[2]{0:T(128)S(1)} %pad_add_fusion.ids_ref, bf16[512,512]{1,0:T(8,128)(2,1)S(1)} %copy-done.2, bf16[4096,512]{1,0:T(8,128)(2,1)S(1)} %copy-done, bf16[1024,128]{1,0:T(8,128)(2,1)S(1)} %get-tuple-element.54.refs_0_, ...), custom_call_target="tpu_custom_call" | custom-call | flops 536870912 | bytes 6291456 | tf_op jit(solution)/shard_map/pallas_call | solution.py:332
  80.5 2.0 %shard_map.137 = (f32[256,512]{1,0:T(8,128)S(1)}, bf16[256,512]{1,0:T(8,128)(2,1)S(1)}, f32[1,256]{1,0:T(1,128)S(1)}) custom-call(s32[8]{0:T(128)S(1)} %copy-done.7, s32[2]{0:T(128)S(1)} %pad_add_fusion.ids_ref, bf16[512,512]{1,0:T(8,128)(2,1)S(1)} %copy-done.2, bf16[4096,512]{1,0:T(8,128)(2,1)S(1)} %copy-done, ...), custom_call_target="tpu_custom_call" | custom-call | flops 1073741824 | bytes 6291456 | tf_op jit(solution)/shard_map/pallas_call | solution.py:332
  82.5 0.0 copy-start.1
  82.5 0.0 copy-start.4
  82.5 3.2 %collective-permute-start.37 = (bf16[256,512]{1,0:T(8,128)(2,1)S(1)}, bf16[256,512]{1,0:T(8,128)(2,1)S(1)}, u32[]{:S(2)}, u32[]{:S(2)}) collective-permute-start(bf16[256,512]{1,0:T(8,128)(2,1)S(1)} %get-tuple-element.51), channel_id=1, source_target_pairs={{0,8},{8,16},{16,24},{24,0},{1,9},{9,17},{17,25},{25,1},{2,10},{10... | collective-permute-start | bytes 786440 | tf_op jit(solution)/shard_map/ppermute | solution.py:560
  85.7 2.0 %shard_map.140 = (f32[256,512]{1,0:T(8,128)S(1)}, bf16[256,512]{1,0:T(8,128)(2,1)}, f32[1,512]{1,0:T(1,128)S(1)}) custom-call(s32[8]{0:T(128)S(1)} %copy-done.7, s32[2]{0:T(128)S(1)} %pad_add_fusion.ids_ref, f32[256,512]{1,0:T(8,128)S(1)} %shard_map.139.base_ref, bf16[4096,512]{1,0:T(8,128)(2,1)S(1)} %copy-done, ...), custom_call_target="tpu_custom_call" | custom-call | flops 536870912 | bytes 6291456 | tf_op jit(solution)/shard_map/pallas_call | solution.py:332
  87.7 1.2 %collective-permute-done.34 = f32[1,512]{1,0:T(1,128)S(1)} collective-permute-done((f32[1,512]{1,0:T(1,128)S(1)}, f32[1,512]{1,0:T(1,128)S(1)}, u32[]{:S(2)}, u32[]{:S(2)}) %collective-permute-start.34) | collective-permute-done | bytes 2080 | tf_op jit(solution)/shard_map/ppermute | solution.py:507
  88.9 2.7 %collective-permute-start.35 = (f32[1,512]{1,0:T(1,128)S(1)}, f32[1,512]{1,0:T(1,128)S(1)}, u32[]{:S(2)}, u32[]{:S(2)}) collective-permute-start(f32[1,512]{1,0:T(1,128)S(1)} %add.17), channel_id=1, source_target_pairs={{0,2},{1,3},{2,0},{3,1},{4,6},{5,7},{6,4},{7,5},{8,10},{9,11},{10,... | collective-permute-start | bytes 6152 | tf_op jit(solution)/shard_map/ppermute | solution.py:507
  91.6 0.1 copy.15.len_ref
  91.8 1.4 %collective-permute-done.35 = f32[1,512]{1,0:T(1,128)S(1)} collective-permute-done((f32[1,512]{1,0:T(1,128)S(1)}, f32[1,512]{1,0:T(1,128)S(1)}, u32[]{:S(2)}, u32[]{:S(2)}) %collective-permute-start.35) | collective-permute-done | bytes 2080 | tf_op jit(solution)/shard_map/ppermute | solution.py:507
  93.2 2.4 %collective-permute-start.36 = (f32[1,512]{1,0:T(1,128)S(1)}, f32[1,512]{1,0:T(1,128)S(1)}, u32[]{:S(2)}, u32[]{:S(2)}) collective-permute-start(f32[1,512]{1,0:T(1,128)S(1)} %add.18), channel_id=1, source_target_pairs={{0,4},{1,5},{2,6},{3,7},{4,0},{5,1},{6,2},{7,3},{8,12},{9,13},{10,... | collective-permute-start | bytes 6152 | tf_op jit(solution)/shard_map/ppermute | solution.py:507
  95.6 0.5 spectrum.1.spec_ref
  96.2 1.5 %collective-permute-done.36 = f32[1,512]{1,0:T(1,128)S(1)} collective-permute-done((f32[1,512]{1,0:T(1,128)S(1)}, f32[1,512]{1,0:T(1,128)S(1)}, u32[]{:S(2)}, u32[]{:S(2)}) %collective-permute-start.36) | collective-permute-done | bytes 2080 | tf_op jit(solution)/shard_map/ppermute | solution.py:507
  97.7 2.0 %collective-permute-start.39 = (f32[1,512]{1,0:T(1,128)S(1)}, f32[1,512]{1,0:T(1,128)S(1)}, u32[]{:S(2)}, u32[]{:S(2)}) collective-permute-start(f32[1,512]{1,0:T(1,128)S(1)} %add.19.sq_ref), channel_id=1, source_target_pairs={{0,8},{8,0},{16,24},{24,16},{1,9},{9,1},{17,25},{25,17},{2,10},{10... | collective-permute-start | bytes 6152 | tf_op jit(solution)/shard_map/ppermute | solution.py:571
  99.7 0.9 collective-permute-start.40
  100.6 2.2 %conv_own.1 = (f32[512,512]{1,0:T(8,128)S(1)}, bf16[256,512]{1,0:T(8,128)(2,1)S(1)}) custom-call(f32[256,512]{1,0:T(8,128)S(1)} %get-tuple-element.37.res_low, f32[256,512]{1,0:T(8,128)S(1)} %get-tuple-element.47.res_high, f32[1,512]{1,0:T(1,128)S(1)} %add.19.sq_ref, f32[512,512]{1,0:T(8,128)S(1)} %spectrum.1.spec_ref, f32[1,512]{1,0:T(1,128)S(1)} %bitcast.5, ...), custom_call_target="tpu_custom_call" | custom-call | flops 671088640 | bytes 3145728 | tf_op jit(solution)/shard_map/conv_own/pallas_call | solution.py:574
  102.8 1.3 %collective-permute-done.40.sq_b = f32[1,512]{1,0:T(1,128)S(1)} collective-permute-done((f32[1,512]{1,0:T(1,128)S(1)}, f32[1,512]{1,0:T(1,128)S(1)}, u32[]{:S(2)}, u32[]{:S(2)}) %collective-permute-start.40) | collective-permute-done | bytes 2080 | tf_op jit(solution)/shard_map/ppermute | solution.py:572
  104.2 2.7 %conv_last.1 = bf16[512,512]{1,0:T(8,128)(2,1)} custom-call(s32[8]{0:T(128)S(1)} %copy-done.7, s32[2]{0:T(128)S(1)} %pad_add_fusion.ids_ref, f32[512,512]{1,0:T(8,128)S(1)} %get-tuple-element.49.part_ref, bf16[256,512]{1,0:T(8,128)(2,1)S(1)} %get-tuple-element.50.low_ref, bf16[256,512]{1,0:T(8,128)(2,1)S(1)} %collective-permute-done.37.raw_low, ...), custom_call_target="tpu_custom_call" | custom-call | flops 671088640 | bytes 3145728 | tf_op jit(solution)/shard_map/conv_last/pallas_call | solution.py:586
  (75 shorter events, 0.5 us)
Async XLA Ops:
  2.0 10.1 %collective-permute-start = (bf16[768,128]{1,0:T(8,128)(2,1)S(1)}, bf16[768,128]{1,0:T(8,128)(2,1)S(1)}, u32[]{:S(2)}, u32[]{:S(2)}) collective-permute-start(bf16[768,128]{1,0:T(8,128)(2,1)S(1)} %get-tuple-element.30), channel_id=1, source_target_pairs={{0,8},{8,0},{16,24},{24,16},{1,9},{9,1},{17,25},{25,17},{2,10},{10... | collective-permute-start | bytes 589832 | tf_op jit(solution)/shard_map/ppermute | solution.py:538
  5.1 11.0 %collective-permute-start.1 = (bf16[768,128]{1,0:T(8,128)(2,1)S(1)}, bf16[768,128]{1,0:T(8,128)(2,1)S(1)}, u32[]{:S(2)}, u32[]{:S(2)}) collective-permute-start(bf16[768,128]{1,0:T(8,128)(2,1)S(1)} %get-tuple-element.31), channel_id=1, source_target_pairs={{0,16},{8,24},{16,0},{24,8},{1,17},{9,25},{17,1},{25,9},{2,18},{10... | collective-permute-start | bytes 589832 | tf_op jit(solution)/shard_map/ppermute | solution.py:538
  6.6 10.0 %collective-permute-start.2 = (bf16[768,128]{1,0:T(8,128)(2,1)S(1)}, bf16[768,128]{1,0:T(8,128)(2,1)S(1)}, u32[]{:S(2)}, u32[]{:S(2)}) collective-permute-start(bf16[768,128]{1,0:T(8,128)(2,1)S(1)} %get-tuple-element.32), channel_id=1, source_target_pairs={{0,24},{8,16},{16,8},{24,0},{1,25},{9,17},{17,9},{25,1},{2,26},{10... | collective-permute-start | bytes 589832 | tf_op jit(solution)/shard_map/ppermute | solution.py:538
  8.6 14.5 %collective-permute-start.17 = (bf16[768,128]{1,0:T(8,128)(2,1)S(1)}, bf16[768,128]{1,0:T(8,128)(2,1)S(1)}, u32[]{:S(2)}, u32[]{:S(2)}) collective-permute-start(bf16[768,128]{1,0:T(8,128)(2,1)S(1)} %get-tuple-element.39), channel_id=1, source_target_pairs={{0,8},{8,0},{16,24},{24,16},{1,9},{9,1},{17,25},{25,17},{2,10},{10... | collective-permute-start | bytes 589832 | tf_op jit(solution)/shard_map/ppermute | solution.py:538
  10.6 14.0 %collective-permute-start.18 = (bf16[768,128]{1,0:T(8,128)(2,1)S(1)}, bf16[768,128]{1,0:T(8,128)(2,1)S(1)}, u32[]{:S(2)}, u32[]{:S(2)}) collective-permute-start(bf16[768,128]{1,0:T(8,128)(2,1)S(1)} %get-tuple-element.40), channel_id=1, source_target_pairs={{0,16},{8,24},{16,0},{24,8},{1,17},{9,25},{17,1},{25,9},{2,18},{10... | collective-permute-start | bytes 589832 | tf_op jit(solution)/shard_map/ppermute | solution.py:538
  12.1 14.2 %collective-permute-start.19 = (bf16[768,128]{1,0:T(8,128)(2,1)S(1)}, bf16[768,128]{1,0:T(8,128)(2,1)S(1)}, u32[]{:S(2)}, u32[]{:S(2)}) collective-permute-start(bf16[768,128]{1,0:T(8,128)(2,1)S(1)} %get-tuple-element.41), channel_id=1, source_target_pairs={{0,24},{8,16},{16,8},{24,0},{1,25},{9,17},{17,9},{25,1},{2,26},{10... | collective-permute-start | bytes 589832 | tf_op jit(solution)/shard_map/ppermute | solution.py:538
  18.9 22.0 %collective-permute-start.7 = (bf16[256,128]{1,0:T(8,128)(2,1)S(1)}, bf16[256,128]{1,0:T(8,128)(2,1)S(1)}, u32[]{:S(2)}, u32[]{:S(2)}) collective-permute-start(bf16[256,128]{1,0:T(8,128)(2,1)S(1)} %get-tuple-element.33), channel_id=1, source_target_pairs={{0,2},{1,3},{2,0},{3,1},{4,6},{5,7},{6,4},{7,5},{8,10},{9,11},{10,... | collective-permute-start | bytes 196616 | tf_op jit(solution)/shard_map/ppermute | solution.py:492
  20.5 23.5 %collective-permute-start.10 = (bf16[256,128]{1,0:T(8,128)(2,1)S(1)}, bf16[256,128]{1,0:T(8,128)(2,1)S(1)}, u32[]{:S(2)}, u32[]{:S(2)}) collective-permute-start(bf16[256,128]{1,0:T(8,128)(2,1)S(1)} %get-tuple-element.33), channel_id=1, source_target_pairs={{0,4},{1,5},{2,6},{3,7},{4,0},{5,1},{6,2},{7,3},{8,12},{9,13},{10,... | collective-permute-start | bytes 196616 | tf_op jit(solution)/shard_map/ppermute | solution.py:492
  23.1 7.2 %collective-permute-start.3 = (bf16[256,128]{1,0:T(8,128)(2,1)S(1)}, bf16[256,128]{1,0:T(8,128)(2,1)S(1)}, u32[]{:S(2)}, u32[]{:S(2)}) collective-permute-start(bf16[256,128]{1,0:T(8,128)(2,1)S(1)} %get-tuple-element.34), channel_id=1, source_target_pairs={{0,8},{8,0},{16,24},{24,16},{1,9},{9,1},{17,25},{25,17},{2,10},{10... | collective-permute-start | bytes 196616 | tf_op jit(solution)/shard_map/ppermute | solution.py:538
  24.6 7.5 %collective-permute-start.4 = (bf16[256,128]{1,0:T(8,128)(2,1)S(1)}, bf16[256,128]{1,0:T(8,128)(2,1)S(1)}, u32[]{:S(2)}, u32[]{:S(2)}) collective-permute-start(bf16[256,128]{1,0:T(8,128)(2,1)S(1)} %get-tuple-element.35), channel_id=1, source_target_pairs={{0,16},{8,24},{16,0},{24,8},{1,17},{9,25},{17,1},{25,9},{2,18},{10... | collective-permute-start | bytes 196616 | tf_op jit(solution)/shard_map/ppermute | solution.py:538
  26.3 7.3 %collective-permute-start.5 = (bf16[256,128]{1,0:T(8,128)(2,1)S(1)}, bf16[256,128]{1,0:T(8,128)(2,1)S(1)}, u32[]{:S(2)}, u32[]{:S(2)}) collective-permute-start(bf16[256,128]{1,0:T(8,128)(2,1)S(1)} %get-tuple-element.36), channel_id=1, source_target_pairs={{0,24},{8,16},{16,8},{24,0},{1,25},{9,17},{17,9},{25,1},{2,26},{10... | collective-permute-start | bytes 196616 | tf_op jit(solution)/shard_map/ppermute | solution.py:538
  26.6 52.5 %copy-start = (bf16[4096,512]{1,0:T(8,128)(2,1)S(1)}, bf16[4096,512]{1,0:T(8,128)(2,1)}, u32[]{:S(2)}) copy-start(bf16[4096,512]{1,0:T(8,128)(2,1)} %w_ref.5) | copy-start | bytes 12582916
  26.6 52.5 %copy-start.2 = (bf16[512,512]{1,0:T(8,128)(2,1)S(1)}, bf16[512,512]{1,0:T(8,128)(2,1)}, u32[]{:S(2)}) copy-start(bf16[512,512]{1,0:T(8,128)(2,1)} %base_ref.3) | copy-start | bytes 1572868
  26.6 52.5 %copy-start.7 = (s32[8]{0:T(128)S(1)}, s32[8]{0:T(128)}, u32[]{:S(2)}) copy-start(s32[8]{0:T(128)} %slots_ref.11) | copy-start | bytes 100
  30.3 7.2 %collective-permute-start.21 = (bf16[256,128]{1,0:T(8,128)(2,1)S(1)}, bf16[256,128]{1,0:T(8,128)(2,1)S(1)}, u32[]{:S(2)}, u32[]{:S(2)}) collective-permute-start(bf16[256,128]{1,0:T(8,128)(2,1)S(1)} %get-tuple-element.44), channel_id=1, source_target_pairs={{0,16},{8,24},{16,0},{24,8},{1,17},{9,25},{17,1},{25,9},{2,18},{10... | collective-permute-start | bytes 196616 | tf_op jit(solution)/shard_map/ppermute | solution.py:538
  32.1 4.3 %collective-permute-start.20 = (bf16[256,128]{1,0:T(8,128)(2,1)S(1)}, bf16[256,128]{1,0:T(8,128)(2,1)S(1)}, u32[]{:S(2)}, u32[]{:S(2)}) collective-permute-start(bf16[256,128]{1,0:T(8,128)(2,1)S(1)} %get-tuple-element.43), channel_id=1, source_target_pairs={{0,8},{8,0},{16,24},{24,16},{1,9},{9,1},{17,25},{25,17},{2,10},{10... | collective-permute-start | bytes 196616 | tf_op jit(solution)/shard_map/ppermute | solution.py:538
  33.7 6.5 %collective-permute-start.22 = (bf16[256,128]{1,0:T(8,128)(2,1)S(1)}, bf16[256,128]{1,0:T(8,128)(2,1)S(1)}, u32[]{:S(2)}, u32[]{:S(2)}) collective-permute-start(bf16[256,128]{1,0:T(8,128)(2,1)S(1)} %get-tuple-element.45), channel_id=1, source_target_pairs={{0,24},{8,16},{16,8},{24,0},{1,25},{9,17},{17,9},{25,1},{2,26},{10... | collective-permute-start | bytes 196616 | tf_op jit(solution)/shard_map/ppermute | solution.py:538
  36.5 30.3 %collective-permute-start.8 = (bf16[768,128]{1,0:T(8,128)(2,1)S(1)}, bf16[768,128]{1,0:T(8,128)(2,1)S(1)}, u32[]{:S(2)}, u32[]{:S(2)}) collective-permute-start(bf16[768,128]{1,0:T(8,128)(2,1)S(1)} %get-tuple-element.61), channel_id=1, source_target_pairs={{0,2},{1,3},{2,0},{3,1},{4,6},{5,7},{6,4},{7,5},{8,10},{9,11},{10,... | collective-permute-start | bytes 589832 | tf_op jit(solution)/shard_map/ppermute | solution.py:492
  37.5 27.8 %collective-permute-start.11 = (bf16[768,128]{1,0:T(8,128)(2,1)S(1)}, bf16[768,128]{1,0:T(8,128)(2,1)S(1)}, u32[]{:S(2)}, u32[]{:S(2)}) collective-permute-start(bf16[768,128]{1,0:T(8,128)(2,1)S(1)} %get-tuple-element.61), channel_id=1, source_target_pairs={{0,4},{1,5},{2,6},{3,7},{4,0},{5,1},{6,2},{7,3},{8,12},{9,13},{10,... | collective-permute-start | bytes 589832 | tf_op jit(solution)/shard_map/ppermute | solution.py:492
  40.2 28.8 %collective-permute-start.14 = (bf16[768,128]{1,0:T(8,128)(2,1)S(1)}, bf16[768,128]{1,0:T(8,128)(2,1)S(1)}, u32[]{:S(2)}, u32[]{:S(2)}) collective-permute-start(bf16[768,128]{1,0:T(8,128)(2,1)S(1)} %get-tuple-element.61), channel_id=1, source_target_pairs={{2,4},{3,5},{4,2},{5,3},{10,12},{11,13},{12,10},{13,11},{18,20},{1... | collective-permute-start | bytes 589832 | tf_op jit(solution)/shard_map/ppermute | solution.py:480
  40.9 7.9 %collective-permute-start.24 = (bf16[512,128]{1,0:T(8,128)(2,1)S(1)}, bf16[512,128]{1,0:T(8,128)(2,1)S(1)}, u32[]{:S(2)}, u32[]{:S(2)}) collective-permute-start(bf16[512,128]{1,0:T(8,128)(2,1)S(1)} %get-tuple-element.57), channel_id=1, source_target_pairs={{0,2},{1,3},{2,0},{3,1},{4,6},{5,7},{6,4},{7,5},{8,10},{9,11},{10,... | collective-permute-start | bytes 393224 | tf_op jit(solution)/shard_map/ppermute | solution.py:492
  44.0 12.6 %collective-permute-start.27 = (bf16[512,128]{1,0:T(8,128)(2,1)S(1)}, bf16[512,128]{1,0:T(8,128)(2,1)S(1)}, u32[]{:S(2)}, u32[]{:S(2)}) collective-permute-start(bf16[512,128]{1,0:T(8,128)(2,1)S(1)} %get-tuple-element.57), channel_id=1, source_target_pairs={{0,4},{1,5},{2,6},{3,7},{4,0},{5,1},{6,2},{7,3},{8,12},{9,13},{10,... | collective-permute-start | bytes 393224 | tf_op jit(solution)/shard_map/ppermute | solution.py:492
  48.8 7.9 %collective-permute-start.25 = (bf16[512,128]{1,0:T(8,128)(2,1)S(1)}, bf16[512,128]{1,0:T(8,128)(2,1)S(1)}, u32[]{:S(2)}, u32[]{:S(2)}) collective-permute-start(bf16[512,128]{1,0:T(8,128)(2,1)S(1)} %get-tuple-element.53), channel_id=1, source_target_pairs={{0,2},{1,3},{2,0},{3,1},{4,6},{5,7},{6,4},{7,5},{8,10},{9,11},{10,... | collective-permute-start | bytes 393224 | tf_op jit(solution)/shard_map/ppermute | solution.py:492
  56.7 7.4 %collective-permute-start.28 = (bf16[512,128]{1,0:T(8,128)(2,1)S(1)}, bf16[512,128]{1,0:T(8,128)(2,1)S(1)}, u32[]{:S(2)}, u32[]{:S(2)}) collective-permute-start(bf16[512,128]{1,0:T(8,128)(2,1)S(1)} %get-tuple-element.53), channel_id=1, source_target_pairs={{0,4},{1,5},{2,6},{3,7},{4,0},{5,1},{6,2},{7,3},{8,12},{9,13},{10,... | collective-permute-start | bytes 393224 | tf_op jit(solution)/shard_map/ppermute | solution.py:492
  56.7 10.0 %collective-permute-start.30 = (bf16[512,128]{1,0:T(8,128)(2,1)S(1)}, bf16[512,128]{1,0:T(8,128)(2,1)S(1)}, u32[]{:S(2)}, u32[]{:S(2)}) collective-permute-start(bf16[512,128]{1,0:T(8,128)(2,1)S(1)} %get-tuple-element.57), channel_id=1, source_target_pairs={{2,4},{3,5},{4,2},{5,3},{10,12},{11,13},{12,10},{13,11},{18,20},{1... | collective-permute-start | bytes 393224 | tf_op jit(solution)/shard_map/ppermute | solution.py:480
  64.0 6.8 %collective-permute-start.31 = (bf16[512,128]{1,0:T(8,128)(2,1)S(1)}, bf16[512,128]{1,0:T(8,128)(2,1)S(1)}, u32[]{:S(2)}, u32[]{:S(2)}) collective-permute-start(bf16[512,128]{1,0:T(8,128)(2,1)S(1)} %collective-permute-done.27), channel_id=1, source_target_pairs={{2,0},{3,1},{4,6},{5,7},{10,8},{11,9},{12,14},{13,15},{18,16},{19,... | collective-permute-start | bytes 393224 | tf_op jit(solution)/shard_map/ppermute | solution.py:482
  65.3 11.9 %collective-permute-start.15 = (bf16[768,128]{1,0:T(8,128)(2,1)S(1)}, bf16[768,128]{1,0:T(8,128)(2,1)S(1)}, u32[]{:S(2)}, u32[]{:S(2)}) collective-permute-start(bf16[768,128]{1,0:T(8,128)(2,1)S(1)} %collective-permute-done.11), channel_id=1, source_target_pairs={{2,0},{3,1},{4,6},{5,7},{10,8},{11,9},{12,14},{13,15},{18,16},{19,... | collective-permute-start | bytes 589832 | tf_op jit(solution)/shard_map/ppermute | solution.py:482
  66.7 11.4 %collective-permute-start.6 = (bf16[1024,128]{1,0:T(8,128)(2,1)S(1)}, bf16[1024,128]{1,0:T(8,128)(2,1)S(1)}, u32[]{:S(2)}, u32[]{:S(2)}) collective-permute-start(bf16[1024,128]{1,0:T(8,128)(2,1)S(1)} %get-tuple-element.62.refs_0_), channel_id=1, source_target_pairs={{0,1},{1,0},{2,3},{3,2},{4,5},{5,4},{6,7},{7,6},{8,9},{9,8},{10,11... | collective-permute-start | bytes 786440 | tf_op jit(solution)/shard_map/ppermute | solution.py:500
  66.8 10.6 %collective-permute-start.13 = (bf16[256,128]{1,0:T(8,128)(2,1)S(1)}, bf16[256,128]{1,0:T(8,128)(2,1)S(1)}, u32[]{:S(2)}, u32[]{:S(2)}) collective-permute-start(bf16[256,128]{1,0:T(8,128)(2,1)S(1)} %get-tuple-element.33), channel_id=1, source_target_pairs={{0,6},{1,7},{2,4},{3,5},{4,2},{5,3},{6,0},{7,1},{8,14},{9,15},{10,... | collective-permute-start | bytes 196616 | tf_op jit(solution)/shard_map/ppermute | solution.py:492
  68.9 9.0 %collective-permute-start.32 = (bf16[512,128]{1,0:T(8,128)(2,1)S(1)}, bf16[512,128]{1,0:T(8,128)(2,1)S(1)}, u32[]{:S(2)}, u32[]{:S(2)}) collective-permute-start(bf16[512,128]{1,0:T(8,128)(2,1)S(1)} %get-tuple-element.53), channel_id=1, source_target_pairs={{0,6},{1,7},{2,4},{3,5},{4,2},{5,3},{6,0},{7,1},{8,14},{9,15},{10,... | collective-permute-start | bytes 393224 | tf_op jit(solution)/shard_map/ppermute | solution.py:492
  70.9 7.7 %collective-permute-start.23 = (bf16[1024,128]{1,0:T(8,128)(2,1)S(1)}, bf16[1024,128]{1,0:T(8,128)(2,1)S(1)}, u32[]{:S(2)}, u32[]{:S(2)}) collective-permute-start(bf16[1024,128]{1,0:T(8,128)(2,1)S(1)} %get-tuple-element.54.refs_0_), channel_id=1, source_target_pairs={{0,1},{1,0},{2,3},{3,2},{4,5},{5,4},{6,7},{7,6},{8,9},{9,8},{10,11... | collective-permute-start | bytes 786440 | tf_op jit(solution)/shard_map/ppermute | solution.py:500
  77.2 1.5 %collective-permute-start.26 = (bf16[1024,128]{1,0:T(8,128)(2,1)S(1)}, bf16[1024,128]{1,0:T(8,128)(2,1)S(1)}, u32[]{:S(2)}, u32[]{:S(2)}) collective-permute-start(bf16[1024,128]{1,0:T(8,128)(2,1)S(1)} %constant_dynamic-update-slice_fusion.19.refs_2_), channel_id=1, source_target_pairs={{0,1},{1,0},{2,3},{3,2},{4,5},{5,4},{6,7},{7,6},{8,9},{9,8},{10,11... | collective-permute-start | bytes 786440 | tf_op jit(solution)/shard_map/ppermute | solution.py:500
  77.4 3.1 %collective-permute-start.9 = (bf16[1024,128]{1,0:T(8,128)(2,1)S(1)}, bf16[1024,128]{1,0:T(8,128)(2,1)S(1)}, u32[]{:S(2)}, u32[]{:S(2)}) collective-permute-start(bf16[1024,128]{1,0:T(8,128)(2,1)S(1)} %constant_dynamic-update-slice_fusion.7.refs_2_), channel_id=1, source_target_pairs={{0,1},{1,0},{2,3},{3,2},{4,5},{5,4},{6,7},{7,6},{8,9},{9,8},{10,11... | collective-permute-start | bytes 786440 | tf_op jit(solution)/shard_map/ppermute | solution.py:500
  78.0 2.5 %collective-permute-start.12 = (bf16[1024,128]{1,0:T(8,128)(2,1)S(1)}, bf16[1024,128]{1,0:T(8,128)(2,1)S(1)}, u32[]{:S(2)}, u32[]{:S(2)}) collective-permute-start(bf16[1024,128]{1,0:T(8,128)(2,1)S(1)} %constant_dynamic-update-slice_fusion.9.refs_4_), channel_id=1, source_target_pairs={{0,1},{1,0},{2,3},{3,2},{4,5},{5,4},{6,7},{7,6},{8,9},{9,8},{10,11... | collective-permute-start | bytes 786440 | tf_op jit(solution)/shard_map/ppermute | solution.py:500
  78.0 2.4 %collective-permute-start.16 = (bf16[1024,128]{1,0:T(8,128)(2,1)S(1)}, bf16[1024,128]{1,0:T(8,128)(2,1)S(1)}, u32[]{:S(2)}, u32[]{:S(2)}) collective-permute-start(bf16[1024,128]{1,0:T(8,128)(2,1)S(1)} %pad_maximum_fusion.refs_6_), channel_id=1, source_target_pairs={{0,1},{1,0},{2,3},{3,2},{4,5},{5,4},{6,7},{7,6},{8,9},{9,8},{10,11... | collective-permute-start | bytes 786440 | tf_op jit(solution)/shard_map/ppermute | solution.py:500
  78.6 7.1 %collective-permute-start.29 = (bf16[1024,128]{1,0:T(8,128)(2,1)S(1)}, bf16[1024,128]{1,0:T(8,128)(2,1)S(1)}, u32[]{:S(2)}, u32[]{:S(2)}) collective-permute-start(bf16[1024,128]{1,0:T(8,128)(2,1)S(1)} %constant_dynamic-update-slice_fusion.21.refs_0_), channel_id=1, source_target_pairs={{0,1},{1,0},{2,3},{3,2},{4,5},{5,4},{6,7},{7,6},{8,9},{9,8},{10,11... | collective-permute-start | bytes 786440 | tf_op jit(solution)/shard_map/ppermute | solution.py:500
  78.7 7.0 %collective-permute-start.33 = (bf16[1024,128]{1,0:T(8,128)(2,1)S(1)}, bf16[1024,128]{1,0:T(8,128)(2,1)S(1)}, u32[]{:S(2)}, u32[]{:S(2)}) collective-permute-start(bf16[1024,128]{1,0:T(8,128)(2,1)S(1)} %pad_maximum_fusion.1.refs_2_), channel_id=1, source_target_pairs={{0,1},{1,0},{2,3},{3,2},{4,5},{5,4},{6,7},{7,6},{8,9},{9,8},{10,11... | collective-permute-start | bytes 786440 | tf_op jit(solution)/shard_map/ppermute | solution.py:500
  82.4 9.2 %copy-start.10 = (s32[512]{0:T(512)S(1)}, s32[512]{0:T(512)}, u32[]{:S(2)}) copy-start(s32[512]{0:T(512)} %param.21) | copy-start | bytes 6148
  82.5 13.2 %copy-start.1 = (bf16[512,256]{1,0:T(8,128)(2,1)S(1)}, bf16[512,256]{1,0:T(8,128)(2,1)}, u32[]{:S(2)}) copy-start(bf16[512,256]{1,0:T(8,128)(2,1)} %constant.16.clone.fh_ref.fh) | copy-start | bytes 786436
  82.5 13.1 %copy-start.4 = (bf16[512,256]{1,0:T(8,128)(2,1)S(1)}, bf16[512,256]{1,0:T(8,128)(2,1)}, u32[]{:S(2)}) copy-start(bf16[512,256]{1,0:T(8,128)(2,1)} %constant.17.clone.fl_ref.fl) | copy-start | bytes 786436
  82.5 13.1 %copy-start.5 = (bf16[512,256]{1,0:T(8,128)(2,1)S(1)}, bf16[512,256]{1,0:T(8,128)(2,1)}, u32[]{:S(2)}) copy-start(bf16[512,256]{1,0:T(8,128)(2,1)} %filters_ref.1) | copy-start | bytes 786436
  82.5 18.1 %copy-start.3 = (bf16[256,512]{1,0:T(8,128)(2,1)S(1)}, bf16[256,512]{1,0:T(8,128)(2,1)}, u32[]{:S(2)}) copy-start(bf16[256,512]{1,0:T(8,128)(2,1)} %constant.18.clone.gh) | copy-start | bytes 786436
  82.5 18.1 %copy-start.6 = (bf16[256,512]{1,0:T(8,128)(2,1)S(1)}, bf16[256,512]{1,0:T(8,128)(2,1)}, u32[]{:S(2)}) copy-start(bf16[256,512]{1,0:T(8,128)(2,1)} %constant.19.clone.gl) | copy-start | bytes 786436
  82.5 18.1 %copy-start.8 = (f32[512]{0:T(512)S(1)}, f32[512]{0:T(512)}, u32[]{:S(2)}) copy-start(f32[512]{0:T(512)} %param.19) | copy-start | bytes 6148
  82.5 18.1 %copy-start.9 = (f32[512]{0:T(512)S(1)}, f32[512]{0:T(512)}, u32[]{:S(2)}) copy-start(f32[512]{0:T(512)} %param.22) | copy-start | bytes 6148
  82.5 21.6 %collective-permute-start.37 = (bf16[256,512]{1,0:T(8,128)(2,1)S(1)}, bf16[256,512]{1,0:T(8,128)(2,1)S(1)}, u32[]{:S(2)}, u32[]{:S(2)}) collective-permute-start(bf16[256,512]{1,0:T(8,128)(2,1)S(1)} %get-tuple-element.51), channel_id=1, source_target_pairs={{0,8},{8,16},{16,24},{24,0},{1,9},{9,17},{17,25},{25,1},{2,10},{10... | collective-permute-start | bytes 786440 | tf_op jit(solution)/shard_map/ppermute | solution.py:560
  87.7 16.4 %collective-permute-start.38 = (bf16[256,512]{1,0:T(8,128)(2,1)}, bf16[256,512]{1,0:T(8,128)(2,1)S(1)}, u32[]{:S(2)}, u32[]{:S(2)}) collective-permute-start(bf16[256,512]{1,0:T(8,128)(2,1)} %get-tuple-element.52), channel_id=1, source_target_pairs={{0,24},{8,0},{16,8},{24,16},{1,25},{9,1},{17,9},{25,17},{2,26},{10... | collective-permute-start | bytes 786440 | tf_op jit(solution)/shard_map/ppermute | solution.py:569
  87.7 1.2 %collective-permute-start.34 = (f32[1,512]{1,0:T(1,128)S(1)}, f32[1,512]{1,0:T(1,128)S(1)}, u32[]{:S(2)}, u32[]{:S(2)}) collective-permute-start(f32[1,512]{1,0:T(1,128)S(1)} %get-tuple-element.48), channel_id=1, source_target_pairs={{0,1},{1,0},{2,3},{3,2},{4,5},{5,4},{6,7},{7,6},{8,9},{9,8},{10,11... | collective-permute-start | bytes 6152 | tf_op jit(solution)/shard_map/ppermute | solution.py:507
  88.9 4.3 %collective-permute-start.35 = (f32[1,512]{1,0:T(1,128)S(1)}, f32[1,512]{1,0:T(1,128)S(1)}, u32[]{:S(2)}, u32[]{:S(2)}) collective-permute-start(f32[1,512]{1,0:T(1,128)S(1)} %add.17), channel_id=1, source_target_pairs={{0,2},{1,3},{2,0},{3,1},{4,6},{5,7},{6,4},{7,5},{8,10},{9,11},{10,... | collective-permute-start | bytes 6152 | tf_op jit(solution)/shard_map/ppermute | solution.py:507
  93.2 4.5 %collective-permute-start.36 = (f32[1,512]{1,0:T(1,128)S(1)}, f32[1,512]{1,0:T(1,128)S(1)}, u32[]{:S(2)}, u32[]{:S(2)}) collective-permute-start(f32[1,512]{1,0:T(1,128)S(1)} %add.18), channel_id=1, source_target_pairs={{0,4},{1,5},{2,6},{3,7},{4,0},{5,1},{6,2},{7,3},{8,12},{9,13},{10,... | collective-permute-start | bytes 6152 | tf_op jit(solution)/shard_map/ppermute | solution.py:507
  97.7 5.2 %collective-permute-start.39 = (f32[1,512]{1,0:T(1,128)S(1)}, f32[1,512]{1,0:T(1,128)S(1)}, u32[]{:S(2)}, u32[]{:S(2)}) collective-permute-start(f32[1,512]{1,0:T(1,128)S(1)} %add.19.sq_ref), channel_id=1, source_target_pairs={{0,8},{8,0},{16,24},{24,16},{1,9},{9,1},{17,25},{25,17},{2,10},{10... | collective-permute-start | bytes 6152 | tf_op jit(solution)/shard_map/ppermute | solution.py:571
  99.7 4.5 %collective-permute-start.40 = (f32[1,512]{1,0:T(1,128)S(1)}, f32[1,512]{1,0:T(1,128)S(1)}, u32[]{:S(2)}, u32[]{:S(2)}) collective-permute-start(f32[1,512]{1,0:T(1,128)S(1)} %add.19.sq_ref), channel_id=1, source_target_pairs={{8,16},{16,8},{24,0},{0,24},{9,17},{17,9},{25,1},{1,25},{10,18},{1... | collective-permute-start | bytes 6152 | tf_op jit(solution)/shard_map/ppermute | solution.py:572
